TPU v7x, 32 devices: a whole 2x2x4 slice. The times are simulated.
32 devices in a mesh: band: 4 (over x, core), mem: 8 (over z, y).
Axes of the slice: x: 2, y: 2, z: 4, core: 2. Of those that a mesh axis runs over, the one named last changes fastest.
Arguments:
- members: bfloat16 [64, 16, 8192], P('band', None, 'mem'), may hold values from -6 to 6
- eigvecs: bfloat16 [112, 16, 8192], P('band', None, 'mem'), may hold values from -6 to 6
- control: float32 [112, 64], replicated, may hold values from -6 to 6
- columns: int32 [512, 16], P('mem'), may hold values from 0 to 1023
- interpolation: bfloat16 [512, 256, 512], P('mem'), may hold values from -0.375 to 0.375
- owners: int32 [512], replicated, may hold values from 0 to 7, as said below
- innovation: float32 [8, 256, 512], P('mem'), may hold values from -6 to 6
- obs_weight: float32 [8, 256, 512], P('mem'), may hold values from 0.25 to 4
Outputs:
- gradient: float32 [112, 64], P(None, 'band')
- departures: float32 [8, 256, 512], P('mem', None, 'band')
Inputs may be any that keep to these rules, and one draw needn't show every extreme that they name: `owners`: one tile sends at most 32 of its blocks to one owner, and some owner holds exactly 32 blocks from every tile.
All inputs are finite; a program needn't handle non-finite values.
Results may differ from a plain program's by a relative error of at most 0.0032.
Values may be sent and summed in bfloat16 or wider, within the bound.
A program may use at most 64 MiB of HBM per device.

v0:
```python
import functools
import math

import jax
import jax.numpy as jnp
from jax import lax
from jax.experimental import pallas as pl
from jax.experimental.pallas import tpu as pltpu
from jax.sharding import PartitionSpec as P

MESH = pl.DeviceIdType.MESH
CHUNKS = 4
VMEM = pl.BlockSpec(memory_space=pltpu.VMEM)


def greet(axes):
    barrier = pltpu.get_barrier_semaphore()
    total = 0
    for axis, size in axes:
        me = lax.axis_index(axis)
        for step in range(1, size):
            pl.semaphore_signal(
                barrier, inc=1, device_id={axis: lax.rem(me + step, size)}, device_id_type=MESH
            )
        total += size - 1
    pl.semaphore_wait(barrier, total)


def remote(src, dst, send, recv, axis, peer):
    return pltpu.make_async_remote_copy(
        src_ref=src, dst_ref=dst, send_sem=send, recv_sem=recv,
        device_id={axis: peer}, device_id_type=MESH,
    )


def spread_part(parts, send, recv, index, rows, size):
    me = lax.axis_index("band")
    copies = []
    for step in range(1, size):
        block = parts.at[me, rows]
        copy = remote(
            block, block, send.at[index, step - 1], recv.at[index, step - 1],
            "band", lax.rem(me + step, size),
        )
        copy.start()
        copies.append(copy)
    return copies


def split(value):
    high = value.astype(jnp.bfloat16)
    return high, (value - high.astype(jnp.float32)).astype(jnp.bfloat16)


def whole_kernel(
    nband, tiles, scale, mem_ref, weight_ref, owners_ref, control_ref,
    eig_hbm, cols_hbm, interp_hbm, innov_hbm, obs_hbm, grad_ref, dep_ref,
    eig_raw, eig_wide, eig_ref, cols_ref, all_ref, mixed, parts, adj_parts, select, interp, innov, obs, image, spread, send, arrived,
    rounded, back, back_own, local, turned, sums,
    load_sem, core_send, core_recv, far_send, far_recv, relay_send, relay_recv,
    part_send, part_recv, out_send, out_recv, back_send, back_recv,
    adj_send, adj_recv, turn_send, turn_recv, sum_send, sum_recv,
):
    me = lax.axis_index("band")
    tile = lax.axis_index("mem")
    levels, mem_dev, tile_cols = mem_ref.shape
    modes_dev = eig_ref.shape[1]
    patch, blocks = cols_ref.shape
    capacity, quarter = send.shape[1:]
    each = levels // CHUNKS
    partner = me + 1 - 2 * lax.rem(me, 2)
    far = lax.rem(me + 2, nband)
    chunks = [pl.ds(c * each, each) for c in range(CHUNKS)]
    whole = pl.ds(0, levels)
    own_obs = pl.ds(pl.multiple_of(me * quarter, quarter), quarter)

    def place(band, rows):
        return all_ref.at[rows, pl.ds(pl.multiple_of(band * mem_dev, mem_dev), mem_dev)]

    own_copy = pltpu.make_async_copy(mem_ref, place(me, whole), load_sem.at[0])
    loads = [
        pltpu.make_async_copy(interp_hbm.at[:, :, own_obs], interp, load_sem.at[1]),
        pltpu.make_async_copy(innov_hbm.at[:, :, own_obs], innov, load_sem.at[2]),
        pltpu.make_async_copy(obs_hbm.at[:, :, own_obs], obs, load_sem.at[3]),
    ]
    eig_copy = pltpu.make_async_copy(eig_hbm, eig_raw, load_sem.at[4])
    cols_copy = pltpu.make_async_copy(cols_hbm, cols_ref, load_sem.at[5])
    eig_copy.start()
    cols_copy.start()
    greet((("band", nband), ("mem", tiles)))
    far_copies = []
    for c, rows in enumerate(chunks):
        copy = remote(
            mem_ref.at[rows], place(me, rows), far_send.at[c], far_recv.at[c], "band", far
        )
        copy.start()
        far_copies.append(copy)
    core_copy = remote(mem_ref, place(me, whole), core_send, core_recv, "band", partner)
    core_copy.start()
    own_copy.start()
    for copy in loads:
        copy.start()

    eig_copy.wait()
    cols_copy.wait()
    eig_wide[...] = eig_raw[...].astype(jnp.float32)
    for level in range(levels):
        eig_ref[level] = eig_wide[:, level, :].astype(jnp.bfloat16)

    def mix(level, carry):
        mixed[level] = jnp.dot(
            weight_ref[...], eig_ref[level], preferred_element_type=jnp.float32
        )
        return carry

    lax.fori_loop(0, levels, mix, 0)
    column = lax.broadcasted_iota(jnp.int32, (patch, tile_cols), 1)
    for j in range(blocks):
        select[j * patch : (j + 1) * patch] = jnp.where(
            cols_ref[:, j : j + 1] == column, 1.0, 0.0
        ).astype(jnp.bfloat16)
    owner = owners_ref[pl.ds(tile, 1)].astype(jnp.float32)
    down = lax.broadcasted_iota(jnp.int32, (blocks, blocks), 0)
    across = lax.broadcasted_iota(jnp.int32, (blocks, blocks), 1)
    owner_column = jnp.sum(jnp.where(down == across, owner, 0.0), axis=1, keepdims=True)
    same = jnp.where(jnp.logical_and(owner_column == owner, down < across), 1.0, 0.0)
    rank = jnp.sum(same, axis=0, keepdims=True)
    target = (owner * capacity + rank).astype(jnp.int32)
    slot = lax.broadcasted_iota(jnp.int32, (tiles * capacity, blocks), 0)
    placing = jnp.where(slot == target, 1.0, 0.0)
    counts = jnp.sum(
        jnp.where(owners_ref[...] == tile, 1.0, 0.0), axis=1, keepdims=True
    ).astype(jnp.int32)
    for copy in loads:
        copy.wait()
    row = lax.broadcasted_iota(jnp.int32, (capacity, quarter), 0)
    for t in range(tiles):
        rows = slice(t * capacity, (t + 1) * capacity)
        obs[0, rows] = jnp.where(row < counts[t : t + 1], 1.0, 0.0) * obs[0, rows]
    own_copy.wait()
    core_copy.wait()
    relays = []

    def relay(c):
        far_copies[c].wait()
        copy = remote(
            place(far, chunks[c]), place(far, chunks[c]), relay_send.at[c], relay_recv.at[c],
            "band", partner,
        )
        copy.start()
        relays.append(copy)

    sends = []
    relay(0)
    for c, rows in enumerate(chunks):
        if c + 1 < CHUNKS:
            relay(c + 1)
        relays[c].wait()
        for i in range(each):
            level = c * each + i
            parts[me, level : level + 1] = jnp.sum(
                all_ref[level].astype(jnp.float32) * mixed[level], axis=0, keepdims=True
            )
        sends += spread_part(parts, part_send, part_recv, c, rows, nband)
    for copy in sends:
        copy.wait()
    total = parts[0]
    for band in range(1, nband):
        total = total + parts[band]
    increment = (scale * total).astype(jnp.bfloat16)

    spread[...] = lax.dot_general(
        select[...], increment, (((1,), (1,)), ((), ())), preferred_element_type=jnp.float32
    )

    def project(j, carry):
        rows = pl.ds(pl.multiple_of(j * patch, patch), patch)
        value = spread[rows]
        total = jnp.zeros((patch, quarter), jnp.float32)
        for level in range(levels):
            total += value[:, level : level + 1] * interp[
                j, level * patch : (level + 1) * patch
            ].astype(jnp.float32)
        image[pl.ds(j, 1)] = jnp.sum(total, axis=0, keepdims=True)
        return carry

    lax.fori_loop(0, blocks, project, 0, unroll=4)
    send[...] = jnp.dot(
        placing, image[...], precision=lax.Precision.HIGHEST, preferred_element_type=jnp.float32
    ).reshape(send.shape)
    outs, backs = [], []
    for step in range(1, tiles):
        peer = lax.rem(tile + step, tiles)
        copy = remote(
            send.at[peer], arrived.at[tile], out_send.at[step - 1], out_recv.at[step - 1],
            "mem", peer,
        )
        copy.start()
        outs.append(copy)

    def depart(source, value):
        rows = pl.ds(pl.multiple_of(source * capacity, capacity), capacity)
        result = obs[0, rows] * (innov[0, rows] - value)
        dep_ref[0, rows] = result
        return result.astype(jnp.bfloat16)

    back_own[...] = depart(tile, send[tile])
    for step in range(1, tiles):
        source = lax.rem(tile + tiles - step, tiles)
        outs[step - 1].wait_recv()
        rounded[source] = depart(source, arrived[source])
        copy = remote(
            rounded.at[source], back.at[tile], back_send.at[step - 1], back_recv.at[step - 1],
            "mem", source,
        )
        copy.start()
        backs.append(copy)
    back[tile] = back_own[...]
    for copy in outs:
        copy.wait_send()
    for copy in backs:
        copy.wait()
    image[...] = lax.dot_general(
        placing.astype(jnp.bfloat16), back[...].reshape(tiles * capacity, quarter),
        (((0,), (0,)), ((), ())), preferred_element_type=jnp.float32,
    )
    lane = lax.broadcasted_iota(jnp.int32, (patch, levels), 1)

    def gather_up(j, carry):
        own = jnp.broadcast_to(image[pl.ds(j, 1)], (levels, quarter)).astype(jnp.bfloat16)
        value = lax.dot_general(
            interp[j], own, (((1,), (1,)), ((), ())), preferred_element_type=jnp.float32
        )
        total = jnp.zeros((patch, levels), jnp.float32)
        for level in range(levels):
            total = jnp.where(lane == level, value[level * patch : (level + 1) * patch], total)
        spread[pl.ds(pl.multiple_of(j * patch, patch), patch)] = total
        return carry

    lax.fori_loop(0, blocks, gather_up, 0, unroll=4)
    high, low = split(spread[...])
    over = (((0,), (0,)), ((), ()))
    adj_parts[me] = lax.dot_general(
        high, select[...], over, preferred_element_type=jnp.float32
    ) + lax.dot_general(low, select[...], over, preferred_element_type=jnp.float32)
    sends = []
    for c, rows in enumerate(chunks):
        sends.append(spread_part(adj_parts, adj_send, adj_recv, c, rows, nband))
    local[...] = jnp.zeros_like(local)
    total = None
    for c in range(CHUNKS):
        for copy in sends[c]:
            copy.wait()
        for i in range(each):
            level = c * each + i
            adjoint = adj_parts[0, level : level + 1]
            for b in range(1, nband):
                adjoint = adjoint + adj_parts[b, level : level + 1]
            weighted = (all_ref[level].astype(jnp.float32) * adjoint).astype(jnp.bfloat16)
            term = lax.dot_general(
                weighted, eig_ref[level], (((1,), (1,)), ((), ())),
                preferred_element_type=jnp.float32,
            )
            total = term if total is None else total + term
    for b in range(nband):
        local[b, :, :modes_dev] = total[b * mem_dev : (b + 1) * mem_dev]
    copies = []
    for step in range(1, nband):
        peer = lax.rem(me + step, nband)
        copy = remote(
            local.at[peer], turned.at[me], turn_send.at[step - 1], turn_recv.at[step - 1],
            "band", peer,
        )
        copy.start()
        copies.append(copy)
    turned[me] = local[me]
    for copy in copies:
        copy.wait()
    own = turned[0]
    for b in range(1, nband):
        own = own + pltpu.roll(turned[b], b * modes_dev, 1)
    sums[tile] = own
    copies = []
    for step in range(1, tiles):
        peer = lax.rem(tile + step, tiles)
        copy = remote(
            sums.at[tile], sums.at[tile], sum_send.at[step - 1], sum_recv.at[step - 1],
            "mem", peer,
        )
        copy.start()
        copies.append(copy)
    for copy in copies:
        copy.wait()
    whole = sums[0]
    for t in range(1, tiles):
        whole = whole + sums[t]
    grad_ref[...] = control_ref[...] - scale * whole[:, : grad_ref.shape[1]]


def dma(*shape):
    return pltpu.SemaphoreType.DMA(shape)


def per_device(members, eigvecs, control, columns, interpolation, owners, innovation, obs_weight):
    nband = lax.axis_size("band")
    tiles = lax.axis_size("mem")
    band_idx = lax.axis_index("band")
    tile_idx = lax.axis_index("mem")
    mem_dev, levels, tile_cols = members.shape
    own_modes = eigvecs.shape[0]
    blocks, patch = columns.shape
    obs_block = interpolation.shape[2]
    capacity = innovation.shape[1] // tiles
    modes, total_members = control.shape
    scale = 1.0 / math.sqrt(modes * total_members)
    quarter = obs_block // nband
    mem_t = jnp.transpose(members, (1, 0, 2))
    weights = lax.dynamic_slice_in_dim(control, band_idx * own_modes, own_modes, 0)
    weights = weights.astype(jnp.bfloat16).T
    own_control = lax.dynamic_slice_in_dim(control, band_idx * mem_dev, mem_dev, 1)
    lanes = pl.cdiv(modes, 128) * 128
    slots = (tiles, capacity, quarter)
    own_slots = (1, tiles * capacity, quarter)
    hbm = pl.BlockSpec(memory_space=pltpu.HBM)
    f32, bf16 = jnp.float32, jnp.bfloat16
    gradient, departure = pl.pallas_call(
        functools.partial(whole_kernel, nband, tiles, scale),
        out_shape=(
            jax.ShapeDtypeStruct((mem_dev, modes), f32),
            jax.ShapeDtypeStruct(own_slots, f32),
        ),
        in_specs=[VMEM] * 4 + [hbm] * 5,
        out_specs=(VMEM, VMEM),
        scratch_shapes=[
            pltpu.VMEM(eigvecs.shape, bf16),
            pltpu.VMEM(eigvecs.shape, f32),
            pltpu.VMEM((levels, own_modes, tile_cols), bf16),
            pltpu.VMEM((patch, blocks), jnp.int32),
            pltpu.VMEM((levels, total_members, tile_cols), bf16),
            pltpu.VMEM((levels, total_members, tile_cols), f32),
            pltpu.VMEM((nband, levels, tile_cols), f32),
            pltpu.VMEM((nband, levels, tile_cols), f32),
            pltpu.VMEM((blocks * patch, tile_cols), bf16),
            pltpu.VMEM((blocks, levels * patch, quarter), bf16),
            pltpu.VMEM(own_slots, f32),
            pltpu.VMEM(own_slots, f32),
            pltpu.VMEM((blocks, quarter), f32),
            pltpu.VMEM((blocks * patch, levels), f32),
            pltpu.VMEM(slots, f32),
            pltpu.VMEM(slots, f32),
            pltpu.VMEM(slots, bf16),
            pltpu.VMEM(slots, bf16),
            pltpu.VMEM((capacity, quarter), bf16),
            pltpu.VMEM((nband, mem_dev, lanes), f32),
            pltpu.VMEM((nband, mem_dev, lanes), f32),
            pltpu.VMEM((tiles, mem_dev, lanes), f32),
            dma(6), dma(), dma(), dma(CHUNKS), dma(CHUNKS), dma(CHUNKS), dma(CHUNKS),
            dma(CHUNKS, nband - 1), dma(CHUNKS, nband - 1),
            dma(tiles - 1), dma(tiles - 1), dma(tiles - 1), dma(tiles - 1),
            dma(CHUNKS, nband - 1), dma(CHUNKS, nband - 1),
            dma(nband - 1), dma(nband - 1), dma(tiles - 1), dma(tiles - 1),
        ],
        compiler_params=pltpu.CompilerParams(
            collective_id=1, has_side_effects=True, vmem_limit_bytes=40 << 20
        ),
    )(
        mem_t, weights, owners.reshape(tiles, blocks), own_control.T,
        *[pltpu.with_memory_space_constraint(x, pltpu.HBM) for x in (eigvecs, columns.T, interpolation, innovation, obs_weight)],
    )
    return (gradient.T, departure)


def solution(mesh):
    return jax.shard_map(
        per_device,
        mesh=mesh,
        in_specs=(
            P("band", None, "mem"),
            P("band", None, "mem"),
            P(),
            P("mem", None),
            P("mem", None, None),
            P(),
            P("mem", None, None),
            P("mem", None, None),
        ),
        out_specs=(P(None, "band"), P("mem", None, "band")),
        check_vma=False,
    )
```

profile of v0, /device:TPU:0, one launch (start us, length us, event | category | flops | bytes accessed | tf_op | source)
XLA Modules:
  0.0 57.8 jit_solution(13860204640932937359)
XLA Ops:
  0.6 0.0 copy-start
  0.7 0.8 %reshape.7.owners_ref = s32[8,64]{1,0:T(8,128)S(1)} reshape(s32[512]{0:T(512)} %param.13) | data formatting | bytes 4096 | tf_op jit(solution)/shard_map/reshape | solution.py:367
  1.4 0.0 copy-done
  1.4 0.1 fusion.weight_ref
  1.5 1.3 %copy.12 = bf16[16,16,1024]{2,0,1:T(8,128)(2,1)S(1)} copy(bf16[16,16,1024]{2,1,0:T(8,128)(2,1)} %param.8) | data formatting | bytes 1048576 | tf_op args[0]
  2.8 53.7 %shard_map.95 = (f32[16,112]{1,0:T(8,128)S(1)}, f32[1,256,128]{2,1,0:T(8,128)S(1)}) custom-call(bf16[16,16,1024]{2,1,0:T(8,128)(2,1)S(1)} %bitcast.9, bf16[64,28]{1,0:T(8,128)(2,1)S(1)} %fusion.weight_ref, s32[8,64]{1,0:T(8,128)S(1)} %reshape.7.owners_ref, f32[16,112]{1,0:T(8,128)S(1)} %dynamic-slice_bitcast_fusion.control_ref, ...), custom_call_target="tpu_custom_call" | custom-call | tf_op jit(solution)/shard_map/pallas_call | solution.py:326
  56.5 0.6 %copy.15 = f32[112,16]{0,1:T(8,128)} copy(f32[112,16]{0,1:T(8,128)S(1)} %bitcast.10) | data formatting | bytes 14336
  57.1 0.7 %copy.16 = f32[1,256,128]{2,1,0:T(8,128)} copy(f32[1,256,128]{2,1,0:T(8,128)S(1)} %get-tuple-element.9) | data formatting | bytes 262144
  (1 shorter events, 0.0 us)
Async XLA Ops:
  0.6 0.8 %copy-start = (f32[112,64]{0,1:T(8,128)S(1)}, f32[112,64]{0,1:T(8,128)}, u32[]{:S(2)}) copy-start(f32[112,64]{0,1:T(8,128)} %param.10) | copy-start | bytes 86020
where the time goes:
time: 58 us; the launch traced here: 57.8 us
  Pallas kernels  53.7 us (93%)
  local copies, waits for them, and re-layouts  3.43 us (6%)
  between operations  0.66 us (1%)
    pallas_call x1, Pallas kernels, per_device(): pl.pallas_call(functools.partial(whole_kernel, nband, tiles, scale), out_...  53.7 us
    unnamed x5, local copies, waits for them, and re-layouts  2.6 us

commit v1 on v0

v1 whole, which is shorter than its diff:
```python
import functools
import math

import jax
import jax.numpy as jnp
from jax import lax
from jax.experimental import pallas as pl
from jax.experimental.pallas import tpu as pltpu
from jax.sharding import PartitionSpec as P

MESH = pl.DeviceIdType.MESH
CORES = 2
CHUNKS = 4
ADJ_CHUNKS = 2
LANES = 128
F32, BF16 = jnp.float32, jnp.bfloat16
HIGHEST = lax.Precision.HIGHEST


def greet(axes):
    barrier = pltpu.get_barrier_semaphore()
    total = 0
    for axis, size in axes:
        me = lax.axis_index(axis)
        for step in range(1, size):
            pl.semaphore_signal(
                barrier, inc=1, device_id={axis: lax.rem(me + step, size)}, device_id_type=MESH
            )
        total += size - 1
    pl.semaphore_wait(barrier, total)


def remote(src, dst, send, recv, axis, peer):
    copy = pltpu.make_async_remote_copy(
        src_ref=src, dst_ref=dst, send_sem=send, recv_sem=recv,
        device_id={axis: peer}, device_id_type=MESH,
    )
    copy.start()
    return copy


def iota(shape, dim):
    return lax.broadcasted_iota(jnp.int32, shape, dim)


def whole_kernel(
    nband, tiles, scale, mem_hbm, eig_hbm, control_hbm, cols_hbm, interp_hbm, owners_hbm,
    innov_hbm, obs_hbm, grad_ref, dep_ref,
    all_ref, eig_all, eig_wide, eig_lvl, control, cols, owners, mixed, mem_wide, mem_lvl,
    base, parts, select, interp, innov, obs, spread, image, send, upward, adj_out, adj_in,
    local, turned, sums,
    load_sem, mem_send, mem_recv, eig_send, eig_recv, far_send, far_recv,
    innov_send, innov_recv, obs_send, obs_recv, part_send, part_recv,
    dep_send, dep_recv, adj_send, adj_recv, turn_send, turn_recv, sum_send, sum_recv,
):
    me = lax.axis_index("band")
    tile = lax.axis_index("mem")
    chips = nband // CORES
    core = lax.rem(me, CORES)
    chip = lax.div(me, CORES)
    members, half, tile_cols = all_ref.shape
    mem_dev = members // nband
    modes_chip = eig_all.shape[0]
    modes_dev = modes_chip // CORES
    levels = half * CORES
    patch, blocks = cols.shape
    capacity, quarter = send.shape[1:]
    partner = me + 1 - 2 * core
    own_obs = pl.ds(pl.multiple_of(me * quarter, quarter), quarter)
    width = tile_cols // CHUNKS
    chunks = [slice(c * width, (c + 1) * width) for c in range(CHUNKS)]

    def halves(which):
        return pl.ds(pl.multiple_of(which * half, half), half)

    own_mem = all_ref.at[pl.ds(me * mem_dev, mem_dev)]
    own_eig = eig_all.at[pl.ds(core * modes_dev, modes_dev)]

    loads = [
        pltpu.make_async_copy(src, dst, load_sem.at[i])
        for i, (src, dst) in enumerate((
            (eig_hbm.at[:, halves(core)], own_eig),
            (control_hbm, control),
            (cols_hbm, cols),
            (owners_hbm, owners),
            (mem_hbm.at[:, halves(core)], own_mem),
            (interp_hbm.at[:, :, own_obs], interp),
            (innov_hbm.at[0, pl.ds(tile * capacity, capacity), own_obs], innov.at[tile]),
            (obs_hbm.at[0, pl.ds(tile * capacity, capacity), own_obs], obs.at[tile]),
        ))
    ]
    for copy in loads[:5]:
        copy.start()
    greet((("band", nband), ("mem", tiles)))
    far_copies = []
    for c, span in enumerate(chunks):
        step_copies = []
        for far in range(1, chips):
            for step in range(CORES):
                target = lax.rem(core + step, CORES)
                peer = lax.rem(chip + far, chips) * CORES + target
                step_copies.append(remote(
                    mem_hbm.at[:, halves(target), span],
                    all_ref.at[pl.ds(me * mem_dev, mem_dev), :, span],
                    far_send.at[c, far - 1, step], far_recv.at[c, far - 1, step], "band", peer,
                ))
        far_copies.append(step_copies)
    eig_copy = remote(
        eig_hbm.at[:, halves(1 - core)], own_eig, eig_send, eig_recv, "band", partner
    )
    mem_copy = remote(
        mem_hbm.at[:, halves(1 - core)], own_mem, mem_send, mem_recv, "band", partner
    )
    early = []
    for step in range(1, tiles):
        peer = lax.rem(tile + step, tiles)
        rows = pl.ds(pl.multiple_of(peer * capacity, capacity), capacity)
        early.append(remote(
            innov_hbm.at[0, rows, own_obs], innov.at[tile], innov_send.at[step - 1],
            innov_recv.at[step - 1], "mem", peer,
        ))
        early.append(remote(
            obs_hbm.at[0, rows, own_obs], obs.at[tile], obs_send.at[step - 1],
            obs_recv.at[step - 1], "mem", peer,
        ))
    for copy in loads[5:]:
        copy.start()
    for copy in loads[:5]:
        copy.wait()

    shape = (members * half, members)
    repeat = jnp.where(lax.div(iota(shape, 0), half) == iota(shape, 1), 1.0, 0.0).astype(BF16)
    rows_of = jnp.dot(repeat, control[...].astype(BF16), preferred_element_type=F32).astype(BF16)
    shape = (control.shape[1], modes_chip * half)
    widen = jnp.where(
        iota(shape, 0) == lax.div(iota(shape, 1), half) + chip * modes_chip, 1.0, 0.0
    ).astype(BF16)
    shape = (members * half, modes_chip * half)
    weight = jnp.where(
        lax.rem(iota(shape, 0), half) == lax.rem(iota(shape, 1), half),
        jnp.dot(rows_of, widen, preferred_element_type=F32), 0.0,
    ).astype(BF16)
    eig_copy.wait()
    for span in chunks:
        wide = eig_all[:, :, span].astype(F32)
        eig_wide[:, :, span] = wide
        mixed[:, :, span] = jnp.dot(
            weight, wide.reshape(modes_chip * half, width).astype(BF16),
            preferred_element_type=F32,
        ).reshape(members, half, width)
    mem_copy.wait()

    def chip_sum(which, span):
        rows = pl.ds(which * (mem_dev * CORES), mem_dev * CORES)
        wide = all_ref[rows, :, span].astype(F32)
        mem_wide[rows, :, span] = wide
        return jnp.sum(wide * mixed[rows, :, span], axis=0)

    for span in chunks:
        base[:, span] = chip_sum(chip, span)
    for level in range(half):
        eig_lvl[level] = eig_wide[:, level, :].astype(BF16)

    per_row = LANES // levels
    groups = blocks // per_row
    column = iota((patch, tile_cols), 1)

    def row_of(j):
        return (lax.rem(j, per_row) * groups + lax.div(j, per_row)) * patch

    for j in range(blocks):
        row = ((j % per_row) * groups + j // per_row) * patch
        select[row : row + patch] = jnp.where(
            cols[:, j : j + 1] == column, 1.0, 0.0
        ).astype(BF16)
    per_lane = owners.shape[1] // blocks
    line = owners[pl.ds(lax.div(tile, per_lane), 1)]
    owner = line[:, :blocks]
    for i in range(1, per_lane):
        owner = jnp.where(
            lax.rem(tile, per_lane) == i, line[:, i * blocks : (i + 1) * blocks], owner
        )
    owner = owner.astype(F32)
    down, across = iota((blocks, blocks), 0), iota((blocks, blocks), 1)
    owner_column = jnp.sum(jnp.where(down == across, owner, 0.0), axis=1, keepdims=True)
    same = jnp.where(jnp.logical_and(owner_column == owner, down < across), 1.0, 0.0)
    rank = jnp.sum(same, axis=0, keepdims=True)
    target = (owner * capacity + rank).astype(jnp.int32)
    placing = jnp.where(iota((tiles * capacity, blocks), 0) == target, 1.0, 0.0)
    for copy in loads[5:]:
        copy.wait()
    for copy in early:
        copy.wait()

    def at_blocks(ref):
        return lax.dot_general(
            placing, ref[...].reshape(tiles * capacity, quarter), (((0,), (0,)), ((), ())),
            precision=HIGHEST, preferred_element_type=F32,
        )

    innov_block = at_blocks(innov)
    obs_block = at_blocks(obs)

    def gather(c):
        span = chunks[c]
        for copy in part_copies[c]:
            copy.wait()
        sides = []
        for side in range(CORES):
            total = parts[side, :, span]
            for other in range(1, chips):
                total = total + parts[other * CORES + side, :, span]
            sides.append((scale * total).astype(BF16).astype(F32))
        increment = jnp.concatenate(sides, axis=0).astype(BF16)
        value = lax.dot_general(
            select[:, span], increment, (((1,), (1,)), ((), ())), preferred_element_type=F32
        )
        if c == 0:
            spread[...] = value
        else:
            spread[...] += value

    part_copies = []
    for c, span in enumerate(chunks):
        for copy in far_copies[c]:
            copy.wait()
        total = base[:, span]
        for far in range(1, chips):
            total = total + chip_sum(lax.rem(chip + far, chips), span)
        parts[me, :, span] = total
        copies = []
        for step in range(1, nband):
            block = parts.at[me, :, span]
            copies.append(remote(
                block, block, part_send.at[c, step - 1], part_recv.at[c, step - 1],
                "band", lax.rem(me + step, nband),
            ))
        part_copies.append(copies)
        if c:
            gather(c - 1)
        for level in range(half):
            mem_lvl[level, :, span] = mem_wide[:, level, span]
    gather(CHUNKS - 1)

    def project(j, carry):
        value = spread[pl.ds(pl.multiple_of(row_of(j), patch), patch)]
        total = jnp.zeros((patch, quarter), F32)
        for level in range(levels):
            total += value[:, level : level + 1] * interp[
                j, level * patch : (level + 1) * patch
            ].astype(F32)
        image[pl.ds(j, 1)] = jnp.sum(total, axis=0, keepdims=True)
        return carry

    lax.fori_loop(0, blocks, project, 0, unroll=4)
    departure = obs_block * (innov_block - image[...])
    image[...] = departure

    lane = iota((patch, LANES), 1)
    turn = lax.rem(lax.div(iota((LANES, quarter), 0), levels), 2)

    def gather_up(g, carry):
        total = jnp.zeros((patch, LANES), F32)
        for pair in range(per_row // 2):
            sides, facing = [], []
            for k in range(2):
                j = g * per_row + 2 * pair + k
                sides.append(interp[j])
                own = jnp.broadcast_to(image[pl.ds(j, 1)], (LANES, quarter))
                facing.append(jnp.where(turn == k, own, 0.0).astype(BF16))
            value = lax.dot_general(
                jnp.concatenate(sides, axis=1), jnp.concatenate(facing, axis=1),
                (((1,), (1,)), ((), ())), preferred_element_type=F32,
            )
            for level in range(levels):
                here = jnp.logical_and(
                    lax.div(lane, 2 * levels) == pair, lax.rem(lane, levels) == level
                )
                total = jnp.where(here, value[level * patch : (level + 1) * patch], total)
        upward[pl.ds(pl.multiple_of(g * patch, patch), patch)] = total
        return carry

    lax.fori_loop(0, groups, gather_up, 0)
    turned_up = upward[...].T
    high = turned_up.astype(BF16)
    low = (turned_up - high.astype(F32)).astype(BF16)
    left = jnp.concatenate([
        jnp.concatenate([x[i * levels : (i + 1) * levels] for i in range(per_row)], axis=1)
        for x in (high, low)
    ], axis=0)
    adj_width = tile_cols // ADJ_CHUNKS
    adj_spans = [slice(c * adj_width, (c + 1) * adj_width) for c in range(ADJ_CHUNKS)]
    adj_copies = []
    for c, span in enumerate(adj_spans):
        value = jnp.dot(left, select[:, span], preferred_element_type=F32)
        value = value[:levels] + value[levels:]
        for side in range(CORES):
            adj_out[side, :, span] = value[side * half : (side + 1) * half]
        copies = []
        for step in range(1, nband):
            peer = lax.rem(me + step, nband)
            copies.append(remote(
                adj_out.at[lax.rem(peer, CORES), :, span], adj_in.at[me, :, span],
                adj_send.at[c, step - 1], adj_recv.at[c, step - 1], "band", peer,
            ))
        adj_copies.append(copies)

    send[...] = jnp.dot(
        placing, image[...], precision=HIGHEST, preferred_element_type=F32
    ).reshape(send.shape)
    own_slots = pl.ds(pl.multiple_of(tile * capacity, capacity), capacity)
    dep_copies = []
    for step in range(1, tiles):
        peer = lax.rem(tile + step, tiles)
        dep_copies.append(remote(
            send.at[peer], dep_ref.at[0, own_slots], dep_send.at[step - 1],
            dep_recv.at[step - 1], "mem", peer,
        ))
    dep_ref[0, own_slots] = send[tile]
    local[...] = jnp.zeros_like(local)

    total = None
    for c, span in enumerate(adj_spans):
        for copy in adj_copies[c]:
            copy.wait()
        adjoint = adj_out[core, :, span]
        for step in range(1, nband):
            adjoint = adjoint + adj_in[lax.rem(me + step, nband), :, span]
        for level in range(half):
            weighted = (mem_lvl[level, :, span] * adjoint[level : level + 1]).astype(BF16)
            term = lax.dot_general(
                weighted, eig_lvl[level, :, span], (((1,), (1,)), ((), ())),
                preferred_element_type=F32,
            )
            total = term if total is None else total + term
    for b in range(nband):
        local[b, :, :modes_chip] = total[b * mem_dev : (b + 1) * mem_dev]
    copies = []
    for step in range(1, nband):
        peer = lax.rem(me + step, nband)
        copies.append(remote(
            local.at[peer], turned.at[me], turn_send.at[step - 1], turn_recv.at[step - 1],
            "band", peer,
        ))
    turned[me] = local[me]
    for copy in copies:
        copy.wait()
    own = None
    for b in range(nband):
        value = turned[b]
        if b >= CORES:
            value = pltpu.roll(value, (b // CORES) * modes_chip, 1)
        own = value if own is None else own + value
    sums[tile] = own
    copies = []
    for step in range(1, tiles):
        peer = lax.rem(tile + step, tiles)
        copies.append(remote(
            sums.at[tile], sums.at[tile], sum_send.at[step - 1], sum_recv.at[step - 1],
            "mem", peer,
        ))
    for copy in copies:
        copy.wait()
    whole = sums[0]
    for t in range(1, tiles):
        whole = whole + sums[t]
    grad_ref[...] = (
        control[pl.ds(pl.multiple_of(me * mem_dev, mem_dev), mem_dev)]
        - scale * whole[:, : grad_ref.shape[1]]
    )
    for copy in dep_copies:
        copy.wait()


def dma(*shape):
    return pltpu.SemaphoreType.DMA(shape)


def per_device(members, eigvecs, control, columns, interpolation, owners, innovation, obs_weight):
    nband = lax.axis_size("band")
    tiles = lax.axis_size("mem")
    mem_dev, levels, tile_cols = members.shape
    own_modes = eigvecs.shape[0]
    blocks, patch = columns.shape
    obs_block = interpolation.shape[2]
    capacity = innovation.shape[1] // tiles
    modes, total_members = control.shape
    scale = 1.0 / math.sqrt(modes * total_members)
    quarter = obs_block // nband
    half = levels // CORES
    chips = nband // CORES
    modes_chip = own_modes * CORES
    group_rows = blocks * levels // LANES * patch
    lanes = pl.cdiv(modes, LANES) * LANES
    slots = (tiles, capacity, quarter)
    own_slots = (1, tiles * capacity, quarter)
    owner_rows = owners.reshape(owners.shape[0] // LANES, LANES)
    hbm = pl.BlockSpec(memory_space=pltpu.HBM)
    vmem = pl.BlockSpec(memory_space=pltpu.VMEM)
    operands = (
        members, eigvecs, control.T, columns.T, interpolation, owner_rows, innovation, obs_weight
    )
    gradient, departure = pl.pallas_call(
        functools.partial(whole_kernel, nband, tiles, scale),
        out_shape=(
            jax.ShapeDtypeStruct((mem_dev, modes), F32),
            jax.ShapeDtypeStruct(own_slots, F32),
        ),
        in_specs=[hbm] * len(operands),
        out_specs=(vmem, vmem),
        scratch_shapes=[
            pltpu.VMEM((total_members, half, tile_cols), BF16),
            pltpu.VMEM((modes_chip, half, tile_cols), BF16),
            pltpu.VMEM((modes_chip, half, tile_cols), F32),
            pltpu.VMEM((half, modes_chip, tile_cols), BF16),
            pltpu.VMEM((total_members, modes), F32),
            pltpu.VMEM((patch, blocks), jnp.int32),
            pltpu.VMEM(owner_rows.shape, jnp.int32),
            pltpu.VMEM((total_members, half, tile_cols), F32),
            pltpu.VMEM((total_members, half, tile_cols), F32),
            pltpu.VMEM((half, total_members, tile_cols), F32),
            pltpu.VMEM((half, tile_cols), F32),
            pltpu.VMEM((nband, half, tile_cols), F32),
            pltpu.VMEM((blocks * patch, tile_cols), BF16),
            pltpu.VMEM((blocks, levels * patch, quarter), BF16),
            pltpu.VMEM(slots, F32),
            pltpu.VMEM(slots, F32),
            pltpu.VMEM((blocks * patch, levels), F32),
            pltpu.VMEM((blocks, quarter), F32),
            pltpu.VMEM(slots, F32),
            pltpu.VMEM((group_rows, LANES), F32),
            pltpu.VMEM((CORES, half, tile_cols), F32),
            pltpu.VMEM((nband, half, tile_cols), F32),
            pltpu.VMEM((nband, mem_dev, lanes), F32),
            pltpu.VMEM((nband, mem_dev, lanes), F32),
            pltpu.VMEM((tiles, mem_dev, lanes), F32),
            dma(8), dma(), dma(), dma(), dma(),
            dma(CHUNKS, chips - 1, CORES), dma(CHUNKS, chips - 1, CORES),
            dma(tiles - 1), dma(tiles - 1), dma(tiles - 1), dma(tiles - 1),
            dma(CHUNKS, nband - 1), dma(CHUNKS, nband - 1),
            dma(tiles - 1), dma(tiles - 1),
            dma(ADJ_CHUNKS, nband - 1), dma(ADJ_CHUNKS, nband - 1),
            dma(nband - 1), dma(nband - 1), dma(tiles - 1), dma(tiles - 1),
        ],
        compiler_params=pltpu.CompilerParams(
            collective_id=1, has_side_effects=True, vmem_limit_bytes=40 << 20
        ),
    )(*[pltpu.with_memory_space_constraint(x, pltpu.HBM) for x in operands])
    return (gradient.T, departure)


def solution(mesh):
    return jax.shard_map(
        per_device,
        mesh=mesh,
        in_specs=(
            P("band", None, "mem"),
            P("band", None, "mem"),
            P(),
            P("mem", None),
            P("mem", None, None),
            P(),
            P("mem", None, None),
            P("mem", None, None),
        ),
        out_specs=(P(None, "band"), P("mem", None, "band")),
        check_vma=False,
    )
```

time: 58 us -> 44.7 us (0.77)
  Pallas kernels: 53.7 us -> 42.6 us
  local copies, waits for them, and re-layouts: 3.43 us -> 1.26 us
    pallas_call x1, Pallas kernels: 53.7 us -> 42.6 us  [per_device(): pl.pallas_call(functools.partial(whole_kernel, nband, tiles, scale), out_...]
    unnamed x5 -> x2, local copies, waits for them, and re-layouts: 2.6 us -> 1.26 us
    reshape x1 -> x0, local copies, waits for them, and re-layouts: 0.76 us -> none  [per_device(): owners.reshape(tiles, blocks)]
where the time goes in v1:
time: 44.7 us; the launch traced here: 44.5 us
  Pallas kernels  42.6 us (95%)
  local copies, waits for them, and re-layouts  1.26 us (3%)
  between operations  0.64 us (1%)
    pallas_call x1, Pallas kernels, per_device(): pl.pallas_call(functools.partial(whole_kernel, nband, tiles, scale), out_...  42.6 us
    unnamed x2, local copies, waits for them, and re-layouts  1.26 us

profile of v1, /device:TPU:0, one launch (start us, length us, event | category | flops | bytes accessed | tf_op | source)
XLA Modules:
  0.0 44.5 jit_solution(17897923391994317159)
XLA Ops:
  0.6 42.6 %shard_map.95 = (f32[16,112]{1,0:T(8,128)S(1)}, f32[1,256,128]{2,1,0:T(8,128)S(1)}) custom-call(bf16[16,16,1024]{2,1,0:T(8,128)(2,1)} %mem_hbm.1, bf16[28,16,1024]{2,1,0:T(8,128)(2,1)} %eig_hbm.1, f32[64,112]{1,0:T(8,128)} %bitcast.5, s32[16,64]{1,0:T(8,128)} %bitcast.6, bf16[64,256,512]{2,1,0:T(8,128)(2,1)} %interp_hbm.1, s32[4,128]{1,0:T(4,128)} %bitcast.7, ...), custom_call_target="tpu_custom_call" | custom-call | tf_op jit(solution)/shard_map/pallas_call | solution.py:403
  43.3 0.6 %copy.12 = f32[112,16]{0,1:T(8,128)} copy(f32[112,16]{0,1:T(8,128)S(1)} %bitcast.4) | data formatting | bytes 14336
  43.9 0.7 %copy.13 = f32[1,256,128]{2,1,0:T(8,128)} copy(f32[1,256,128]{2,1,0:T(8,128)S(1)} %get-tuple-element.9) | data formatting | bytes 262144

commit v2 on v1

v2 whole, which is shorter than its diff:
```python
import functools
import math

import jax
import jax.numpy as jnp
from jax import lax
from jax.experimental import pallas as pl
from jax.experimental.pallas import tpu as pltpu
from jax.sharding import PartitionSpec as P

MESH = pl.DeviceIdType.MESH
CORES = 2
SUB = 8
DEPTH = 256
SPANS = 2
AHEAD = 2
LANES = 128
F32, BF16 = jnp.float32, jnp.bfloat16
HIGHEST = lax.Precision.HIGHEST


def flip(index, bit):
    return index + bit * (1 - 2 * lax.rem(lax.div(index, bit), 2))


def signal(semaphore, axis, peer):
    pl.semaphore_signal(semaphore, inc=1, device_id={axis: peer}, device_id_type=MESH)


def remote(src, dst, send, recv, axis, peer):
    copy = pltpu.make_async_remote_copy(
        src_ref=src, dst_ref=dst, send_sem=send, recv_sem=recv,
        device_id={axis: peer}, device_id_type=MESH,
    )
    copy.start()
    return copy


def iota(shape, dim):
    return lax.broadcasted_iota(jnp.int32, shape, dim)


def whole_kernel(
    nband, tiles, scale, mem_hbm, eig_hbm, control_hbm, cols_hbm, interp_hbm, owners_hbm,
    innov_hbm, obs_hbm, grad_ref, dep_ref,
    all_ref, eig_all, eig_wide, eig_lvl, control, cols, owners, mixed, mem_wide, mem_lvl,
    base, parts, select, interp, innov, obs, spread, image, send, upward, adj_out, adj_in,
    local, turned, sums, meet,
    load_sem, mem_send, mem_recv, eig_send, eig_recv, far_send, far_recv,
    innov_send, innov_recv, obs_send, obs_recv, part_send, part_recv,
    dep_send, dep_recv, adj_send, adj_recv, turn_send, turn_recv, sum_send, sum_recv,
):
    me = lax.axis_index("band")
    tile = lax.axis_index("mem")
    chips = nband // CORES
    core = lax.rem(me, CORES)
    chip = lax.div(me, CORES)
    subs, members, _, half = all_ref.shape
    mem_dev = members // nband
    mem_chip = mem_dev * CORES
    modes_chip = eig_all.shape[1]
    modes_dev = modes_chip // CORES
    levels = subs * SUB
    patch, blocks = cols.shape
    capacity, quarter = send.shape[1:]
    rounds = meet.shape[0]
    partner = me + 1 - 2 * core
    own_obs = pl.ds(pl.multiple_of(me * quarter, quarter), quarter)
    width = half // SPANS
    spans = [slice(c * width, (c + 1) * width) for c in range(SPANS)]
    chunks = [(sub, span) for sub in range(subs) for span in spans]

    def rows_of_sub(sub):
        return slice(sub * SUB, (sub + 1) * SUB)

    def columns_of(which, span=slice(0, None)):
        start = span.start
        size = (half if span.stop is None else span.stop) - start
        return pl.ds(pl.multiple_of(which * half + start, size), size)

    own_mem = pl.ds(me * mem_dev, mem_dev)
    own_eig = pl.ds(core * modes_dev, modes_dev)

    pairs = [
        (eig_hbm.at[:, rows_of_sub(sub), columns_of(core)], eig_all.at[sub, own_eig])
        for sub in range(subs)
    ] + [(control_hbm, control), (cols_hbm, cols), (owners_hbm, owners)] + [
        (mem_hbm.at[:, rows_of_sub(sub), columns_of(core)], all_ref.at[sub, own_mem])
        for sub in range(subs)
    ] + [
        (interp_hbm.at[:, :, own_obs], interp),
        (innov_hbm.at[0, pl.ds(tile * capacity, capacity), own_obs], innov.at[tile]),
        (obs_hbm.at[0, pl.ds(tile * capacity, capacity), own_obs], obs.at[tile]),
    ]
    loads = [
        pltpu.make_async_copy(src, dst, load_sem.at[i]) for i, (src, dst) in enumerate(pairs)
    ]
    late = len(loads) - 3
    for copy in loads[:late]:
        copy.start()

    barrier = pltpu.get_barrier_semaphore()
    for step in range(1, nband):
        signal(barrier, "band", lax.rem(me + step, nband))
    for i in range(rounds):
        signal(barrier, "mem", flip(tile, 1 << i))
    pl.semaphore_wait(barrier, nband - 1 + rounds)

    far_copies = []

    def send_members(c):
        sub, span = chunks[c]
        copies = []
        for far in range(1, chips):
            for step in range(CORES):
                target = lax.rem(core + step, CORES)
                peer = lax.rem(chip + far, chips) * CORES + target
                copies.append(remote(
                    mem_hbm.at[:, rows_of_sub(sub), columns_of(target, span)],
                    all_ref.at[sub, own_mem, :, span],
                    far_send.at[c, far - 1, step], far_recv.at[c, far - 1, step], "band", peer,
                ))
        far_copies.append(copies)

    for c in range(AHEAD):
        send_members(c)
    eig_copies = [
        remote(
            eig_hbm.at[:, rows_of_sub(sub), columns_of(1 - core)], eig_all.at[sub, own_eig],
            eig_send.at[sub], eig_recv.at[sub], "band", partner,
        )
        for sub in range(subs)
    ]
    mem_copies = [
        remote(
            mem_hbm.at[:, rows_of_sub(sub), columns_of(1 - core)], all_ref.at[sub, own_mem],
            mem_send.at[sub], mem_recv.at[sub], "band", partner,
        )
        for sub in range(subs)
    ]
    for copy in loads[late:]:
        copy.start()
    for i in range(rounds):
        signal(meet.at[i], "mem", flip(tile, 1 << i))
        pl.semaphore_wait(meet.at[i], 1)
    early = []
    for step in range(1, tiles):
        peer = lax.rem(tile + step, tiles)
        rows = pl.ds(pl.multiple_of(peer * capacity, capacity), capacity)
        early.append(remote(
            innov_hbm.at[0, rows, own_obs], innov.at[tile], innov_send.at[step - 1],
            innov_recv.at[step - 1], "mem", peer,
        ))
        early.append(remote(
            obs_hbm.at[0, rows, own_obs], obs.at[tile], obs_send.at[step - 1],
            obs_recv.at[step - 1], "mem", peer,
        ))
    for copy in loads[:late]:
        copy.wait()

    shape = (members * SUB, members)
    repeat = jnp.where(lax.div(iota(shape, 0), SUB) == iota(shape, 1), 1.0, 0.0).astype(BF16)
    rows_of = jnp.dot(repeat, control[...].astype(BF16), preferred_element_type=F32).astype(BF16)
    shape = (control.shape[1], modes_chip * SUB)
    widen = jnp.where(
        iota(shape, 0) == lax.div(iota(shape, 1), SUB) + chip * modes_chip, 1.0, 0.0
    ).astype(BF16)
    shape = (members * SUB, modes_chip * SUB)
    weight = jnp.where(
        lax.rem(iota(shape, 0), SUB) == lax.rem(iota(shape, 1), SUB),
        jnp.dot(rows_of, widen, preferred_element_type=F32), 0.0,
    ).astype(BF16)

    def chip_sum(which, sub, span):
        rows = pl.ds(which * mem_chip, mem_chip)
        wide = all_ref[sub, rows, :, span].astype(F32)
        mem_wide[sub, rows, :, span] = wide
        return jnp.sum(wide * mixed[sub, rows, :, span], axis=0)

    for sub in range(subs):
        eig_copies[sub].wait()
        mem_copies[sub].wait()
        for span in spans:
            wide = eig_all[sub, :, :, span].astype(F32)
            eig_wide[sub, :, :, span] = wide
            mixed[sub, :, :, span] = jnp.dot(
                weight, wide.reshape(modes_chip * SUB, width).astype(BF16),
                preferred_element_type=F32,
            ).reshape(members, SUB, width)
            base[sub, :, span] = chip_sum(chip, sub, span)

    column = iota((patch, half * CORES), 1)
    for j in range(blocks):
        select[j * patch : (j + 1) * patch] = jnp.where(
            cols[:, j : j + 1] == column, 1.0, 0.0
        ).astype(BF16)

    part_copies = []

    def finish(c):
        sub, span = chunks[c]
        for copy in far_copies[c]:
            copy.wait()
        total = base[sub, :, span]
        for far in range(1, chips):
            total = total + chip_sum(lax.rem(chip + far, chips), sub, span)
        parts[me, sub, :, span] = total
        copies = []
        for step in range(1, nband):
            block = parts.at[me, sub, :, span]
            copies.append(remote(
                block, block, part_send.at[c, step - 1], part_recv.at[c, step - 1],
                "band", lax.rem(me + step, nband),
            ))
        part_copies.append(copies)
        if c + AHEAD < len(chunks):
            send_members(c + AHEAD)

    def gather(c):
        sub, span = chunks[c]
        for copy in part_copies[c]:
            copy.wait()
        value = None
        for side in range(CORES):
            total = parts[side, sub, :, span]
            for other in range(1, chips):
                total = total + parts[other * CORES + side, sub, :, span]
            term = lax.dot_general(
                (scale * total).astype(BF16),
                select[:, side * half + span.start : side * half + span.stop],
                (((1,), (1,)), ((), ())), preferred_element_type=F32,
            )
            value = term if value is None else value + term
        if span.start == 0:
            spread[rows_of_sub(sub)] = value
        else:
            spread[rows_of_sub(sub)] += value

    per_group = DEPTH // patch
    groups = blocks // per_group
    diagonal = lax.div(iota((per_group, DEPTH), 1), patch) == iota((per_group, DEPTH), 0)

    def blocks_of(group, level):
        return jnp.concatenate([
            interp[
                group * per_group : (group + 1) * per_group, at * patch : (at + 1) * patch
            ].reshape(DEPTH, quarter)
            for at in (level, level + 1)
        ], axis=1)

    def project(sub):
        for group in range(groups):
            lanes = slice(group * DEPTH, (group + 1) * DEPTH)
            total = None
            for level in range(sub * SUB, (sub + 1) * SUB, 2):
                left = jnp.concatenate([
                    jnp.where(diagonal, spread[at : at + 1, lanes], 0.0)
                    for at in (level, level + 1)
                ], axis=0).astype(BF16)
                term = jnp.dot(left, blocks_of(group, level), preferred_element_type=F32)
                total = term if total is None else total + term
            value = total[:per_group, :quarter] + total[per_group:, quarter:]
            rows = slice(group * per_group, (group + 1) * per_group)
            if sub == 0:
                image[rows] = value
            else:
                image[rows] += value

    def spread_members(c):
        sub, span = chunks[c]
        for level in range(SUB):
            mem_lvl[sub * SUB + level, :, span] = mem_wide[sub, :, level, span]

    finish(0)
    for sub in range(subs):
        for level in range(SUB):
            eig_lvl[sub * SUB + level] = eig_wide[sub, :, level, :].astype(BF16)
    spread_members(0)

    finish(1)
    per_lane = owners.shape[1] // blocks
    line = owners[pl.ds(lax.div(tile, per_lane), 1)]
    owner = line[:, :blocks]
    for i in range(1, per_lane):
        owner = jnp.where(
            lax.rem(tile, per_lane) == i, line[:, i * blocks : (i + 1) * blocks], owner
        )
    owner = owner.astype(F32)
    down, across = iota((blocks, blocks), 0), iota((blocks, blocks), 1)
    owner_column = jnp.sum(jnp.where(down == across, owner, 0.0), axis=1, keepdims=True)
    same = jnp.where(jnp.logical_and(owner_column == owner, down < across), 1.0, 0.0)
    rank = jnp.sum(same, axis=0, keepdims=True)
    target = (owner * capacity + rank).astype(jnp.int32)
    placing = jnp.where(iota((tiles * capacity, blocks), 0) == target, 1.0, 0.0)
    for copy in loads[late:]:
        copy.wait()
    for copy in early:
        copy.wait()

    def at_blocks(ref):
        return lax.dot_general(
            placing, ref[...].reshape(tiles * capacity, quarter), (((0,), (0,)), ((), ())),
            precision=HIGHEST, preferred_element_type=F32,
        )

    innov_block = at_blocks(innov)
    obs_block = at_blocks(obs)
    gather(0)
    spread_members(1)

    done = 0
    for c in range(2, len(chunks)):
        finish(c)
        gather(c - 1)
        if chunks[c - 1][0] != chunks[c][0]:
            project(chunks[c - 1][0])
            done = chunks[c][0]
        spread_members(c)
    gather(len(chunks) - 1)
    project(done)
    departure = obs_block * (innov_block - image[...])
    image[...] = departure

    rounded = departure.astype(BF16)
    blank = jnp.zeros((per_group, quarter), BF16)
    for group in range(groups):
        own = rounded[group * per_group : (group + 1) * per_group]
        left = jnp.concatenate([
            jnp.concatenate([own, blank], axis=1), jnp.concatenate([blank, own], axis=1)
        ], axis=0)
        for level in range(0, levels, 2):
            value = lax.dot_general(
                left, blocks_of(group, level), (((1,), (1,)), ((), ())),
                preferred_element_type=F32,
            )
            for k in range(2):
                upward[level + k : level + k + 1, group * DEPTH : (group + 1) * DEPTH] = jnp.sum(
                    jnp.where(diagonal, value[k * per_group : (k + 1) * per_group], 0.0),
                    axis=0, keepdims=True,
                )
    high = upward[...].astype(BF16)
    low = (upward[...] - high.astype(F32)).astype(BF16)
    left = jnp.concatenate([high, low], axis=0)
    far_peers = [lax.rem(chip + far, chips) * CORES for far in range(1, chips)]
    adj_copies = []
    for c, span in enumerate(spans):
        copies = []
        for own in range(CORES):
            side = core if own else 1 - core
            value = jnp.dot(
                left, select[:, columns_of(side, span)], preferred_element_type=F32
            )
            adj_out[own, :, span] = value[:levels] + value[levels:]
            peers = [peer + side for peer in far_peers]
            if not own:
                peers = [partner] + peers
            for peer in peers:
                k = len(copies)
                copies.append(remote(
                    adj_out.at[own, :, span], adj_in.at[k, :, span],
                    adj_send.at[c, k], adj_recv.at[c, k], "band", peer,
                ))
        adj_copies.append(copies)

    send[...] = jnp.dot(
        placing, image[...], precision=HIGHEST, preferred_element_type=F32
    ).reshape(send.shape)
    own_slots = pl.ds(pl.multiple_of(tile * capacity, capacity), capacity)
    dep_copies = []
    for step in range(1, tiles):
        peer = lax.rem(tile + step, tiles)
        dep_copies.append(remote(
            send.at[peer], dep_ref.at[0, own_slots], dep_send.at[step - 1],
            dep_recv.at[step - 1], "mem", peer,
        ))
    dep_ref[0, own_slots] = send[tile]
    local[...] = jnp.zeros_like(local)

    total = None
    for c, span in enumerate(spans):
        for copy in adj_copies[c]:
            copy.wait()
        adjoint = adj_out[1, :, span]
        for k in range(nband - 1):
            adjoint = adjoint + adj_in[k, :, span]
        for level in range(levels):
            weighted = (mem_lvl[level, :, span] * adjoint[level : level + 1]).astype(BF16)
            term = lax.dot_general(
                weighted, eig_lvl[level, :, span], (((1,), (1,)), ((), ())),
                preferred_element_type=F32,
            )
            total = term if total is None else total + term
    for b in range(nband):
        local[b, :, :modes_chip] = total[b * mem_dev : (b + 1) * mem_dev]
    copies = []
    for step in range(1, nband):
        peer = lax.rem(me + step, nband)
        copies.append(remote(
            local.at[peer], turned.at[me], turn_send.at[step - 1], turn_recv.at[step - 1],
            "band", peer,
        ))
    turned[me] = local[me]
    for copy in copies:
        copy.wait()
    own = None
    for b in range(nband):
        value = turned[b]
        if b >= CORES:
            value = pltpu.roll(value, (b // CORES) * modes_chip, 1)
        own = value if own is None else own + value
    sums[tile] = own
    copies = []
    for step in range(1, tiles):
        peer = lax.rem(tile + step, tiles)
        copies.append(remote(
            sums.at[tile], sums.at[tile], sum_send.at[step - 1], sum_recv.at[step - 1],
            "mem", peer,
        ))
    for copy in copies:
        copy.wait()
    whole = sums[0]
    for t in range(1, tiles):
        whole = whole + sums[t]
    grad_ref[...] = (
        control[pl.ds(pl.multiple_of(me * mem_dev, mem_dev), mem_dev)]
        - scale * whole[:, : grad_ref.shape[1]]
    )
    for copy in dep_copies:
        copy.wait()


def dma(*shape):
    return pltpu.SemaphoreType.DMA(shape)


def per_device(members, eigvecs, control, columns, interpolation, owners, innovation, obs_weight):
    nband = lax.axis_size("band")
    tiles = lax.axis_size("mem")
    mem_dev, levels, tile_cols = members.shape
    own_modes = eigvecs.shape[0]
    blocks, patch = columns.shape
    obs_block = interpolation.shape[2]
    capacity = innovation.shape[1] // tiles
    modes, total_members = control.shape
    scale = 1.0 / math.sqrt(modes * total_members)
    quarter = obs_block // nband
    half = tile_cols // CORES
    subs = levels // SUB
    chips = nband // CORES
    modes_chip = own_modes * CORES
    rounds = (tiles - 1).bit_length()
    lanes = pl.cdiv(modes, LANES) * LANES
    slots = (tiles, capacity, quarter)
    own_slots = (1, tiles * capacity, quarter)
    owner_rows = owners.reshape(owners.shape[0] // LANES, LANES)
    hbm = pl.BlockSpec(memory_space=pltpu.HBM)
    vmem = pl.BlockSpec(memory_space=pltpu.VMEM)
    operands = (
        members, eigvecs, control.T, columns.T, interpolation, owner_rows, innovation, obs_weight
    )
    gradient, departure = pl.pallas_call(
        functools.partial(whole_kernel, nband, tiles, scale),
        out_shape=(
            jax.ShapeDtypeStruct((mem_dev, modes), F32),
            jax.ShapeDtypeStruct(own_slots, F32),
        ),
        in_specs=[hbm] * len(operands),
        out_specs=(vmem, vmem),
        scratch_shapes=[
            pltpu.VMEM((subs, total_members, SUB, half), BF16),
            pltpu.VMEM((subs, modes_chip, SUB, half), BF16),
            pltpu.VMEM((subs, modes_chip, SUB, half), F32),
            pltpu.VMEM((levels, modes_chip, half), BF16),
            pltpu.VMEM((total_members, modes), F32),
            pltpu.VMEM((patch, blocks), jnp.int32),
            pltpu.VMEM(owner_rows.shape, jnp.int32),
            pltpu.VMEM((subs, total_members, SUB, half), F32),
            pltpu.VMEM((subs, total_members, SUB, half), F32),
            pltpu.VMEM((levels, total_members, half), F32),
            pltpu.VMEM((subs, SUB, half), F32),
            pltpu.VMEM((nband, subs, SUB, half), F32),
            pltpu.VMEM((blocks * patch, tile_cols), BF16),
            pltpu.VMEM((blocks, levels * patch, quarter), BF16),
            pltpu.VMEM(slots, F32),
            pltpu.VMEM(slots, F32),
            pltpu.VMEM((levels, blocks * patch), F32),
            pltpu.VMEM((blocks, quarter), F32),
            pltpu.VMEM(slots, F32),
            pltpu.VMEM((levels, blocks * patch), F32),
            pltpu.VMEM((CORES, levels, half), F32),
            pltpu.VMEM((nband - 1, levels, half), F32),
            pltpu.VMEM((nband, mem_dev, lanes), F32),
            pltpu.VMEM((nband, mem_dev, lanes), F32),
            pltpu.VMEM((tiles, mem_dev, lanes), F32),
            pltpu.SemaphoreType.REGULAR((rounds,)),
            dma(6 + 2 * subs), dma(subs), dma(subs), dma(subs), dma(subs),
            dma(subs * SPANS, chips - 1, CORES), dma(subs * SPANS, chips - 1, CORES),
            dma(tiles - 1), dma(tiles - 1), dma(tiles - 1), dma(tiles - 1),
            dma(subs * SPANS, nband - 1), dma(subs * SPANS, nband - 1),
            dma(tiles - 1), dma(tiles - 1),
            dma(SPANS, nband - 1), dma(SPANS, nband - 1),
            dma(nband - 1), dma(nband - 1), dma(tiles - 1), dma(tiles - 1),
        ],
        compiler_params=pltpu.CompilerParams(
            collective_id=1, has_side_effects=True, vmem_limit_bytes=40 << 20
        ),
    )(*[pltpu.with_memory_space_constraint(x, pltpu.HBM) for x in operands])
    return (gradient.T, departure)


def solution(mesh):
    return jax.shard_map(
        per_device,
        mesh=mesh,
        in_specs=(
            P("band", None, "mem"),
            P("band", None, "mem"),
            P(),
            P("mem", None),
            P("mem", None, None),
            P(),
            P("mem", None, None),
            P("mem", None, None),
        ),
        out_specs=(P(None, "band"), P("mem", None, "band")),
        check_vma=False,
    )
```

time: 44.7 us -> 37.9 us (0.85)
  Pallas kernels: 42.6 us -> 35.9 us
    pallas_call x1, Pallas kernels: 42.6 us -> 35.9 us  [per_device(): pl.pallas_call(functools.partial(whole_kernel, nband, tiles, scale), out_...]
where the time goes in v2:
time: 37.9 us; the launch traced here: 37.8 us
  Pallas kernels  35.9 us (95%)
  local copies, waits for them, and re-layouts  1.26 us (3%)
  between operations  0.64 us (2%)
    pallas_call x1, Pallas kernels, per_device(): pl.pallas_call(functools.partial(whole_kernel, nband, tiles, scale), out_...  35.9 us
    unnamed x2, local copies, waits for them, and re-layouts  1.26 us

profile of v2, /device:TPU:0, one launch (start us, length us, event | category | flops | bytes accessed | tf_op | source)
XLA Modules:
  0.0 37.8 jit_solution(5132325155421410020)
XLA Ops:
  0.6 35.9 %shard_map.95 = (f32[16,112]{1,0:T(8,128)S(1)}, f32[1,256,128]{2,1,0:T(8,128)S(1)}) custom-call(bf16[16,16,1024]{2,1,0:T(8,128)(2,1)} %mem_hbm.1, bf16[28,16,1024]{2,1,0:T(8,128)(2,1)} %eig_hbm.1, f32[64,112]{1,0:T(8,128)} %bitcast.5, s32[16,64]{1,0:T(8,128)} %bitcast.6, bf16[64,256,512]{2,1,0:T(8,128)(2,1)} %interp_hbm.1, s32[4,128]{1,0:T(4,128)} %bitcast.7, ...), custom_call_target="tpu_custom_call" | custom-call | tf_op jit(solution)/shard_map/pallas_call | solution.py:461
  36.5 0.6 %copy.12 = f32[112,16]{0,1:T(8,128)} copy(f32[112,16]{0,1:T(8,128)S(1)} %bitcast.4) | data formatting | bytes 14336
  37.1 0.7 %copy.13 = f32[1,256,128]{2,1,0:T(8,128)} copy(f32[1,256,128]{2,1,0:T(8,128)S(1)} %get-tuple-element.9) | data formatting | bytes 262144

commit v3 on v2

--- a/solution.py
+++ b/solution.py
@@ -13,27 +13,41 @@
 SUB = 8
 DEPTH = 256
 SPANS = 2
-AHEAD = 2
 LANES = 128
 F32, BF16 = jnp.float32, jnp.bfloat16
 HIGHEST = lax.Precision.HIGHEST
 
 
-def flip(index, bit):
-    return index + bit * (1 - 2 * lax.rem(lax.div(index, bit), 2))
+def snake(index):
+    row, column = lax.div(index, 2), lax.rem(index, 2)
+    return index + lax.rem(row, 2) * (1 - 2 * column)
 
 
 def signal(semaphore, axis, peer):
     pl.semaphore_signal(semaphore, inc=1, device_id={axis: peer}, device_id_type=MESH)
 
 
-def remote(src, dst, send, recv, axis, peer):
-    copy = pltpu.make_async_remote_copy(
+def signal_beside(semaphore, place, reach, size):
+    def inform(there):
+        @pl.when(jnp.logical_and(there >= 0, there < size))
+        def _():
+            signal(semaphore, "mem", snake(there))
+
+    inform(place - reach)
+    inform(place + reach)
+    below = jnp.where(place >= reach, 1, 0)
+    return below + jnp.where(place + reach < size, 1, 0)
+
+
+def await_bytes(ref, semaphore):
+    pltpu.make_async_copy(ref, ref, semaphore).wait()
+
+
+def remote(src, dst, send, recv, **device):
+    pltpu.make_async_remote_copy(
         src_ref=src, dst_ref=dst, send_sem=send, recv_sem=recv,
-        device_id={axis: peer}, device_id_type=MESH,
-    )
-    copy.start()
-    return copy
+        device_id=device, device_id_type=MESH,
+    ).start()
 
 
 def iota(shape, dim):
@@ -45,10 +59,11 @@
     innov_hbm, obs_hbm, grad_ref, dep_ref,
     all_ref, eig_all, eig_wide, eig_lvl, control, cols, owners, mixed, mem_wide, mem_lvl,
     base, parts, select, interp, innov, obs, spread, image, send, upward, adj_out, adj_in,
-    local, turned, sums, meet,
-    load_sem, mem_send, mem_recv, eig_send, eig_recv, far_send, far_recv,
-    innov_send, innov_recv, obs_send, obs_recv, part_send, part_recv,
-    dep_send, dep_recv, adj_send, adj_recv, turn_send, turn_recv, sum_send, sum_recv,
+    local, packed, terms, meet,
+    load_sem, mem_recv, eig_recv, far_recv, part_recv, adj_recv,
+    innov_recv, obs_recv, dep_recv, sum_recv,
+    mem_send, eig_send, far_send, part_send, adj_send,
+    innov_send, obs_send, dep_send, sum_send,
 ):
     me = lax.axis_index("band")
     tile = lax.axis_index("mem")
@@ -81,82 +96,72 @@
     own_mem = pl.ds(me * mem_dev, mem_dev)
     own_eig = pl.ds(core * modes_dev, modes_dev)
 
-    pairs = [
-        (eig_hbm.at[:, rows_of_sub(sub), columns_of(core)], eig_all.at[sub, own_eig])
-        for sub in range(subs)
-    ] + [(control_hbm, control), (cols_hbm, cols), (owners_hbm, owners)] + [
-        (mem_hbm.at[:, rows_of_sub(sub), columns_of(core)], all_ref.at[sub, own_mem])
-        for sub in range(subs)
-    ] + [
-        (interp_hbm.at[:, :, own_obs], interp),
-        (innov_hbm.at[0, pl.ds(tile * capacity, capacity), own_obs], innov.at[tile]),
-        (obs_hbm.at[0, pl.ds(tile * capacity, capacity), own_obs], obs.at[tile]),
+    loads = [
+        (eig_all.at[:, own_eig], [
+            (eig_hbm.at[:, rows_of_sub(sub), columns_of(core)], eig_all.at[sub, own_eig])
+            for sub in range(subs)
+        ]),
+        (control, [(control_hbm, control)]),
+        (cols, [(cols_hbm, cols)]),
+        (owners, [(owners_hbm, owners)]),
+        (all_ref.at[:, own_mem], [
+            (mem_hbm.at[:, rows_of_sub(sub), columns_of(core)], all_ref.at[sub, own_mem])
+            for sub in range(subs)
+        ]),
+        (interp, [(interp_hbm.at[:, :, own_obs], interp)]),
+        (innov.at[tile], [
+            (innov_hbm.at[0, pl.ds(tile * capacity, capacity), own_obs], innov.at[tile])
+        ]),
+        (obs.at[tile], [
+            (obs_hbm.at[0, pl.ds(tile * capacity, capacity), own_obs], obs.at[tile])
+        ]),
     ]
-    loads = [
-        pltpu.make_async_copy(src, dst, load_sem.at[i]) for i, (src, dst) in enumerate(pairs)
-    ]
+
+    def load(which):
+        for i in which:
+            for src, dst in loads[i][1]:
+                pltpu.make_async_copy(src, dst, load_sem.at[i]).start()
+
+    def loaded(which):
+        for i in which:
+            await_bytes(loads[i][0], load_sem.at[i])
+
     late = len(loads) - 3
-    for copy in loads[:late]:
-        copy.start()
+    load(range(late))
 
     barrier = pltpu.get_barrier_semaphore()
     for step in range(1, nband):
         signal(barrier, "band", lax.rem(me + step, nband))
-    for i in range(rounds):
-        signal(barrier, "mem", flip(tile, 1 << i))
-    pl.semaphore_wait(barrier, nband - 1 + rounds)
-
-    far_copies = []
+    place = snake(tile)
+    heard = signal_beside(barrier, place, 1, tiles)
+    pl.semaphore_wait(barrier, nband - 1 + heard)
 
     def send_members(c):
         sub, span = chunks[c]
-        copies = []
         for far in range(1, chips):
             for step in range(CORES):
                 target = lax.rem(core + step, CORES)
                 peer = lax.rem(chip + far, chips) * CORES + target
-                copies.append(remote(
+                remote(
                     mem_hbm.at[:, rows_of_sub(sub), columns_of(target, span)],
-                    all_ref.at[sub, own_mem, :, span],
-                    far_send.at[c, far - 1, step], far_recv.at[c, far - 1, step], "band", peer,
-                ))
-        far_copies.append(copies)
-
-    for c in range(AHEAD):
+                    all_ref.at[sub, own_mem, :, span], far_send, far_recv.at[c], band=peer,
+                )
+
+    for c in range(len(chunks)):
         send_members(c)
-    eig_copies = [
+    for sub in range(subs):
         remote(
             eig_hbm.at[:, rows_of_sub(sub), columns_of(1 - core)], eig_all.at[sub, own_eig],
-            eig_send.at[sub], eig_recv.at[sub], "band", partner,
-        )
-        for sub in range(subs)
-    ]
-    mem_copies = [
+            eig_send, eig_recv.at[sub], band=partner,
+        )
+    for sub in range(subs):
         remote(
             mem_hbm.at[:, rows_of_sub(sub), columns_of(1 - core)], all_ref.at[sub, own_mem],
-            mem_send.at[sub], mem_recv.at[sub], "band", partner,
-        )
-        for sub in range(subs)
-    ]
-    for copy in loads[late:]:
-        copy.start()
-    for i in range(rounds):
-        signal(meet.at[i], "mem", flip(tile, 1 << i))
-        pl.semaphore_wait(meet.at[i], 1)
-    early = []
-    for step in range(1, tiles):
-        peer = lax.rem(tile + step, tiles)
-        rows = pl.ds(pl.multiple_of(peer * capacity, capacity), capacity)
-        early.append(remote(
-            innov_hbm.at[0, rows, own_obs], innov.at[tile], innov_send.at[step - 1],
-            innov_recv.at[step - 1], "mem", peer,
-        ))
-        early.append(remote(
-            obs_hbm.at[0, rows, own_obs], obs.at[tile], obs_send.at[step - 1],
-            obs_recv.at[step - 1], "mem", peer,
-        ))
-    for copy in loads[:late]:
-        copy.wait()
+            mem_send, mem_recv.at[sub], band=partner,
+        )
+    load(range(late, len(loads)))
+    heard = signal_beside(meet.at[0], place, 1, tiles)
+    loaded(range(late))
 
     shape = (members * SUB, members)
     repeat = jnp.where(lax.div(iota(shape, 0), SUB) == iota(shape, 1), 1.0, 0.0).astype(BF16)
@@ -171,6 +176,13 @@
         jnp.dot(rows_of, widen, preferred_element_type=F32), 0.0,
     ).astype(BF16)
 
+    def meet_next(i, heard):
+        pl.semaphore_wait(meet.at[i], heard)
+        if i + 1 < rounds:
+            return signal_beside(meet.at[i + 1], place, 1 << (i + 1), tiles)
+
+    heard = meet_next(0, heard)
+
     def chip_sum(which, sub, span):
         rows = pl.ds(which * mem_chip, mem_chip)
         wide = all_ref[sub, rows, :, span].astype(F32)
@@ -178,8 +190,8 @@
         return jnp.sum(wide * mixed[sub, rows, :, span], axis=0)
 
     for sub in range(subs):
-        eig_copies[sub].wait()
-        mem_copies[sub].wait()
+        await_bytes(eig_all.at[sub, own_eig], eig_recv.at[sub])
+        await_bytes(all_ref.at[sub, own_mem], mem_recv.at[sub])
         for span in spans:
             wide = eig_all[sub, :, :, span].astype(F32)
             eig_wide[sub, :, :, span] = wide
@@ -189,37 +201,39 @@
             ).reshape(members, SUB, width)
             base[sub, :, span] = chip_sum(chip, sub, span)
 
+    heard = meet_next(1, heard)
     column = iota((patch, half * CORES), 1)
     for j in range(blocks):
         select[j * patch : (j + 1) * patch] = jnp.where(
             cols[:, j : j + 1] == column, 1.0, 0.0
         ).astype(BF16)
 
-    part_copies = []
+    for i in range(2, rounds):
+        heard = meet_next(i, heard)
+    for step in range(1, tiles):
+        peer = lax.rem(tile + step, tiles)
+        rows = pl.ds(pl.multiple_of(peer * capacity, capacity), capacity)
+        remote(
+            innov_hbm.at[0, rows, own_obs], innov.at[tile], innov_send, innov_recv, mem=peer
+        )
+        remote(obs_hbm.at[0, rows, own_obs], obs.at[tile], obs_send, obs_recv, mem=peer)
 
     def finish(c):
         sub, span = chunks[c]
-        for copy in far_copies[c]:
-            copy.wait()
+        await_bytes(all_ref.at[sub, : members - mem_chip, :, span], far_recv.at[c])
         total = base[sub, :, span]
         for far in range(1, chips):
             total = total + chip_sum(lax.rem(chip + far, chips), sub, span)
         parts[me, sub, :, span] = total
-        copies = []
         for step in range(1, nband):
             block = parts.at[me, sub, :, span]
-            copies.append(remote(
-                block, block, part_send.at[c, step - 1], part_recv.at[c, step - 1],
-                "band", lax.rem(me + step, nband),
-            ))
-        part_copies.append(copies)
-        if c + AHEAD < len(chunks):
-            send_members(c + AHEAD)
+            remote(
+                block, block, part_send, part_recv.at[c], band=lax.rem(me + step, nband)
+            )
 
     def gather(c):
         sub, span = chunks[c]
-        for copy in part_copies[c]:
-            copy.wait()
+        await_bytes(parts.at[: nband - 1, sub, :, span], part_recv.at[c])
         value = None
         for side in range(CORES):
             total = parts[side, sub, :, span]
@@ -277,7 +291,9 @@
             eig_lvl[sub * SUB + level] = eig_wide[sub, :, level, :].astype(BF16)
     spread_members(0)
 
-    finish(1)
+    for c in range(1, len(chunks) - 1):
+        finish(c)
+        spread_members(c)
     per_lane = owners.shape[1] // blocks
     line = owners[pl.ds(lax.div(tile, per_lane), 1)]
     owner = line[:, :blocks]
@@ -292,10 +308,10 @@
     rank = jnp.sum(same, axis=0, keepdims=True)
     target = (owner * capacity + rank).astype(jnp.int32)
     placing = jnp.where(iota((tiles * capacity, blocks), 0) == target, 1.0, 0.0)
-    for copy in loads[late:]:
-        copy.wait()
-    for copy in early:
-        copy.wait()
+    loaded(range(late, len(loads)))
+    others = slice(0, tiles - 1)
+    await_bytes(innov.at[others], innov_recv)
+    await_bytes(obs.at[others], obs_recv)
 
     def at_blocks(ref):
         return lax.dot_general(
@@ -305,19 +321,13 @@
 
     innov_block = at_blocks(innov)
     obs_block = at_blocks(obs)
-    gather(0)
-    spread_members(1)
-
-    done = 0
-    for c in range(2, len(chunks)):
-        finish(c)
-        gather(c - 1)
-        if chunks[c - 1][0] != chunks[c][0]:
-            project(chunks[c - 1][0])
-            done = chunks[c][0]
-        spread_members(c)
-    gather(len(chunks) - 1)
-    project(done)
+    finish(len(chunks) - 1)
+    for sub in range(subs):
+        for c in range(sub * SPANS, (sub + 1) * SPANS):
+            if c == len(chunks) - 1:
+                spread_members(c)
+            gather(c)
+        project(sub)
     departure = obs_block * (innov_block - image[...])
     image[...] = departure
 
@@ -342,44 +352,42 @@
     low = (upward[...] - high.astype(F32)).astype(BF16)
     left = jnp.concatenate([high, low], axis=0)
     far_peers = [lax.rem(chip + far, chips) * CORES for far in range(1, chips)]
-    adj_copies = []
     for c, span in enumerate(spans):
-        copies = []
+        value = jnp.dot(
+            left,
+            jnp.concatenate([
+                select[:, columns_of(side, span)] for side in (1 - core, core)
+            ], axis=1),
+            preferred_element_type=F32,
+        )
+        value = value[:levels] + value[levels:]
+        k = 0
         for own in range(CORES):
             side = core if own else 1 - core
-            value = jnp.dot(
-                left, select[:, columns_of(side, span)], preferred_element_type=F32
-            )
-            adj_out[own, :, span] = value[:levels] + value[levels:]
+            adj_out[own, :, span] = value[:, own * width : (own + 1) * width]
             peers = [peer + side for peer in far_peers]
             if not own:
-                peers = [partner] + peers
+                peers = [*peers, partner]
             for peer in peers:
-                k = len(copies)
-                copies.append(remote(
+                remote(
                     adj_out.at[own, :, span], adj_in.at[k, :, span],
-                    adj_send.at[c, k], adj_recv.at[c, k], "band", peer,
-                ))
-        adj_copies.append(copies)
+                    adj_send, adj_recv.at[c], band=peer,
+                )
+                k += 1
 
     send[...] = jnp.dot(
         placing, image[...], precision=HIGHEST, preferred_element_type=F32
     ).reshape(send.shape)
     own_slots = pl.ds(pl.multiple_of(tile * capacity, capacity), capacity)
-    dep_copies = []
     for step in range(1, tiles):
         peer = lax.rem(tile + step, tiles)
-        dep_copies.append(remote(
-            send.at[peer], dep_ref.at[0, own_slots], dep_send.at[step - 1],
-            dep_recv.at[step - 1], "mem", peer,
-        ))
+        remote(send.at[peer], dep_ref.at[0, own_slots], dep_send, dep_recv, mem=peer)
     dep_ref[0, own_slots] = send[tile]
     local[...] = jnp.zeros_like(local)
 
     total = None
     for c, span in enumerate(spans):
-        for copy in adj_copies[c]:
-            copy.wait()
+        await_bytes(adj_in.at[:, :, span], adj_recv.at[c])
         adjoint = adj_out[1, :, span]
         for k in range(nband - 1):
             adjoint = adjoint + adj_in[k, :, span]
@@ -390,43 +398,49 @@
                 preferred_element_type=F32,
             )
             total = term if total is None else total + term
+    local[:, :modes_chip] = total
+    rows = mem_dev // 2
     for b in range(nband):
-        local[b, :, :modes_chip] = total[b * mem_dev : (b + 1) * mem_dev]
-    copies = []
-    for step in range(1, nband):
-        peer = lax.rem(me + step, nband)
-        copies.append(remote(
-            local.at[peer], turned.at[me], turn_send.at[step - 1], turn_recv.at[step - 1],
-            "band", peer,
-        ))
-    turned[me] = local[me]
-    for copy in copies:
-        copy.wait()
-    own = None
-    for b in range(nband):
-        value = turned[b]
-        if b >= CORES:
-            value = pltpu.roll(value, (b // CORES) * modes_chip, 1)
-        own = value if own is None else own + value
-    sums[tile] = own
-    copies = []
-    for step in range(1, tiles):
-        peer = lax.rem(tile + step, tiles)
-        copies.append(remote(
-            sums.at[tile], sums.at[tile], sum_send.at[step - 1], sum_recv.at[step - 1],
-            "mem", peer,
-        ))
-    for copy in copies:
-        copy.wait()
-    whole = sums[0]
-    for t in range(1, tiles):
-        whole = whole + sums[t]
+        packed[b] = local[b * mem_dev : b * mem_dev + rows] + pltpu.roll(
+            local[b * mem_dev + rows : (b + 1) * mem_dev], LANES // 2, 1
+        )
+    for far in range(tiles - 1, -1, -1):
+        for step in range(nband - 1, -1, -1):
+            if far or step:
+                peer = lax.rem(me + step, nband)
+                remote(
+                    packed.at[peer], terms.at[me, tile], sum_send, sum_recv,
+                    band=peer, mem=lax.rem(tile + far, tiles),
+                )
+    terms[me, tile] = packed[me]
+    sums = terms.reshape(nband * tiles, rows, LANES)
+    peers = nband * tiles - 1
+    await_bytes(sums.at[:peers], sum_recv)
+    whole = [jnp.zeros((rows, LANES), F32)] * 2
+    lane = iota((rows, LANES), 1)
+    for c in range(chips):
+        value = terms[c * CORES, 0]
+        for t in range(1, tiles * CORES):
+            value = value + terms[c * CORES + t // tiles, t % tiles]
+        for k in range(2):
+            turned = value if k == 0 else pltpu.roll(value, LANES // 2, 1)
+            turned = jnp.where(lane < modes_chip, turned, 0.0)
+            whole[k] = whole[k] + (pltpu.roll(turned, c * modes_chip, 1) if c else turned)
+    whole = jnp.concatenate(whole, axis=0)
     grad_ref[...] = (
         control[pl.ds(pl.multiple_of(me * mem_dev, mem_dev), mem_dev)]
         - scale * whole[:, : grad_ref.shape[1]]
     )
-    for copy in dep_copies:
-        copy.wait()
+    await_bytes(dep_ref.at[0, : (tiles - 1) * capacity], dep_recv)
+    sent = (
+        (mem_hbm, far_send), (eig_all.at[:, own_eig], eig_send),
+        (all_ref.at[:, own_mem], mem_send), (innov.at[others], innov_send),
+        (obs.at[others], obs_send), (parts.at[: nband - 1], part_send), (adj_in, adj_send),
+        (send.at[others], dep_send), (sums.at[:peers], sum_send),
+    )
+    for ref, semaphore in sent:
+        for _ in range(chips - 1 if semaphore is far_send else 1):
+            await_bytes(ref, semaphore)
 
 
 def dma(*shape):
@@ -449,7 +463,6 @@
     chips = nband // CORES
     modes_chip = own_modes * CORES
     rounds = (tiles - 1).bit_length()
-    lanes = pl.cdiv(modes, LANES) * LANES
     slots = (tiles, capacity, quarter)
     own_slots = (1, tiles * capacity, quarter)
     owner_rows = owners.reshape(owners.shape[0] // LANES, LANES)
@@ -489,17 +502,12 @@
             pltpu.VMEM((levels, blocks * patch), F32),
             pltpu.VMEM((CORES, levels, half), F32),
             pltpu.VMEM((nband - 1, levels, half), F32),
-            pltpu.VMEM((nband, mem_dev, lanes), F32),
-            pltpu.VMEM((nband, mem_dev, lanes), F32),
-            pltpu.VMEM((tiles, mem_dev, lanes), F32),
+            pltpu.VMEM((total_members, LANES), F32),
+            pltpu.VMEM((nband, mem_dev // 2, LANES), F32),
+            pltpu.VMEM((nband, tiles, mem_dev // 2, LANES), F32),
             pltpu.SemaphoreType.REGULAR((rounds,)),
-            dma(6 + 2 * subs), dma(subs), dma(subs), dma(subs), dma(subs),
-            dma(subs * SPANS, chips - 1, CORES), dma(subs * SPANS, chips - 1, CORES),
-            dma(tiles - 1), dma(tiles - 1), dma(tiles - 1), dma(tiles - 1),
-            dma(subs * SPANS, nband - 1), dma(subs * SPANS, nband - 1),
-            dma(tiles - 1), dma(tiles - 1),
-            dma(SPANS, nband - 1), dma(SPANS, nband - 1),
-            dma(nband - 1), dma(nband - 1), dma(tiles - 1), dma(tiles - 1),
+            dma(8), dma(subs), dma(subs), dma(subs * SPANS), dma(subs * SPANS), dma(SPANS),
+            *[dma() for _ in range(13)],
         ],
         compiler_params=pltpu.CompilerParams(
             collective_id=1, has_side_effects=True, vmem_limit_bytes=40 << 20

time: 37.9 us -> 35.8 us (0.945)
  Pallas kernels: 35.9 us -> 33.7 us
    pallas_call x1, Pallas kernels: 35.9 us -> 33.7 us  [per_device(): pl.pallas_call(functools.partial(whole_kernel, nband, tiles, scale), out_...]
where the time goes in v3:
time: 35.8 us; the launch traced here: 35.6 us
  Pallas kernels  33.7 us (94%)
  local copies, waits for them, and re-layouts  1.26 us (4%)
  between operations  0.64 us (2%)
    pallas_call x1, Pallas kernels, per_device(): pl.pallas_call(functools.partial(whole_kernel, nband, tiles, scale), out_...  33.7 us
    unnamed x2, local copies, waits for them, and re-layouts  1.26 us

profile of v3, /device:TPU:0, one launch (start us, length us, event | category | flops | bytes accessed | tf_op | source)
XLA Modules:
  0.0 35.6 jit_solution(14506538964865204654)
XLA Ops:
  0.6 33.7 %shard_map.95 = (f32[16,112]{1,0:T(8,128)S(1)}, f32[1,256,128]{2,1,0:T(8,128)S(1)}) custom-call(bf16[16,16,1024]{2,1,0:T(8,128)(2,1)} %mem_hbm.1, bf16[28,16,1024]{2,1,0:T(8,128)(2,1)} %eig_hbm.1, f32[64,112]{1,0:T(8,128)} %bitcast.5, s32[16,64]{1,0:T(8,128)} %bitcast.6, bf16[64,256,512]{2,1,0:T(8,128)(2,1)} %interp_hbm.1, s32[4,128]{1,0:T(4,128)} %bitcast.7, ...), custom_call_target="tpu_custom_call" | custom-call | tf_op jit(solution)/shard_map/pallas_call | solution.py:474
  34.4 0.6 %copy.12 = f32[112,16]{0,1:T(8,128)} copy(f32[112,16]{0,1:T(8,128)S(1)} %bitcast.4) | data formatting | bytes 14336
  35.0 0.7 %copy.13 = f32[1,256,128]{2,1,0:T(8,128)} copy(f32[1,256,128]{2,1,0:T(8,128)S(1)} %get-tuple-element.9) | data formatting | bytes 262144

commit v4 on v3

--- a/solution.py
+++ b/solution.py
@@ -308,10 +308,7 @@
     rank = jnp.sum(same, axis=0, keepdims=True)
     target = (owner * capacity + rank).astype(jnp.int32)
     placing = jnp.where(iota((tiles * capacity, blocks), 0) == target, 1.0, 0.0)
-    loaded(range(late, len(loads)))
     others = slice(0, tiles - 1)
-    await_bytes(innov.at[others], innov_recv)
-    await_bytes(obs.at[others], obs_recv)
 
     def at_blocks(ref):
         return lax.dot_general(
@@ -319,13 +316,17 @@
             precision=HIGHEST, preferred_element_type=F32,
         )
 
-    innov_block = at_blocks(innov)
-    obs_block = at_blocks(obs)
+    loaded([late])
     finish(len(chunks) - 1)
     for sub in range(subs):
         for c in range(sub * SPANS, (sub + 1) * SPANS):
             if c == len(chunks) - 1:
                 spread_members(c)
+                loaded(range(late + 1, len(loads)))
+                await_bytes(innov.at[others], innov_recv)
+                await_bytes(obs.at[others], obs_recv)
+                innov_block = at_blocks(innov)
+                obs_block = at_blocks(obs)
             gather(c)
         project(sub)
     departure = obs_block * (innov_block - image[...])
@@ -441,6 +442,15 @@
     for ref, semaphore in sent:
         for _ in range(chips - 1 if semaphore is far_send else 1):
             await_bytes(ref, semaphore)
+
+
+def write_out(grad_ref, dep_ref, grad_out, dep_out, sem):
+    pairs = ((dep_ref, dep_out), (grad_ref, grad_out))
+    copies = [pltpu.make_async_copy(*pair, sem.at[i]) for i, pair in enumerate(pairs)]
+    for copy in copies:
+        copy.start()
+    for copy in copies:
+        copy.wait()
 
 
 def dma(*shape):
@@ -513,6 +523,14 @@
             collective_id=1, has_side_effects=True, vmem_limit_bytes=40 << 20
         ),
     )(*[pltpu.with_memory_space_constraint(x, pltpu.HBM) for x in operands])
+    results = (gradient, departure)
+    gradient, departure = pl.pallas_call(
+        write_out,
+        out_shape=tuple(jax.ShapeDtypeStruct(x.shape, x.dtype) for x in results),
+        in_specs=[vmem, vmem],
+        out_specs=(hbm, hbm),
+        scratch_shapes=[dma(2)],
+    )(*[pltpu.with_memory_space_constraint(x, pltpu.VMEM) for x in results])
     return (gradient.T, departure)
 
 

time: 35.8 us -> 34.7 us (0.969)
  local copies, waits for them, and re-layouts: 1.26 us -> 0 us
    unnamed x2 -> x0, local copies, waits for them, and re-layouts: 1.26 us -> none
    pallas_call x0 -> x1, Pallas kernels: none -> 0.68 us  [per_device(): pl.pallas_call(write_out, out_shape=tuple((jax.ShapeDtypeStruct(x.shape,...]
    pallas_call x1, Pallas kernels: 33.7 us -> 33.2 us  [per_device(): pl.pallas_call(functools.partial(whole_kernel, nband, tiles, scale), out_...]
where the time goes in v4:
time: 34.7 us; the launch traced here: 34.6 us
  Pallas kernels  33.9 us (98%)
  between operations  0.64 us (2%)
    pallas_call x1, Pallas kernels, per_device(): pl.pallas_call(functools.partial(whole_kernel, nband, tiles, scale), out_...  33.2 us

profile of v4, /device:TPU:0, one launch (start us, length us, event | category | flops | bytes accessed | tf_op | source)
XLA Modules:
  0.0 34.6 jit_solution(8481191401624720610)
XLA Ops:
  0.6 33.2 %shard_map.95 = (f32[16,112]{1,0:T(8,128)S(1)}, f32[1,256,128]{2,1,0:T(8,128)S(1)}) custom-call(bf16[16,16,1024]{2,1,0:T(8,128)(2,1)} %mem_hbm.1, bf16[28,16,1024]{2,1,0:T(8,128)(2,1)} %eig_hbm.1, f32[64,112]{1,0:T(8,128)} %bitcast.4, s32[16,64]{1,0:T(8,128)} %bitcast.5, bf16[64,256,512]{2,1,0:T(8,128)(2,1)} %interp_hbm.1, s32[4,128]{1,0:T(4,128)} %bitcast.6, ...), custom_call_target="tpu_custom_call" | custom-call | tf_op jit(solution)/shard_map/pallas_call | solution.py:484
  33.9 0.7 %shard_map.96 = (f32[16,112]{1,0:T(8,128)}, f32[1,256,128]{2,1,0:T(8,128)}) custom-call(f32[16,112]{1,0:T(8,128)S(1)} %get-tuple-element.6.grad_ref, f32[1,256,128]{2,1,0:T(8,128)S(1)} %get-tuple-element.7.dep_ref), custom_call_target="tpu_custom_call" | custom-call | tf_op jit(solution)/shard_map/pallas_call | solution.py:527

commit v5 on v4

--- a/solution.py
+++ b/solution.py
@@ -59,7 +59,7 @@
     innov_hbm, obs_hbm, grad_ref, dep_ref,
     all_ref, eig_all, eig_wide, eig_lvl, control, cols, owners, mixed, mem_wide, mem_lvl,
     base, parts, select, interp, innov, obs, spread, image, send, upward, adj_out, adj_in,
-    local, packed, terms, meet,
+    local, packed, terms, turned, meet,
     load_sem, mem_recv, eig_recv, far_recv, part_recv, adj_recv,
     innov_recv, obs_recv, dep_recv, sum_recv,
     mem_send, eig_send, far_send, part_send, adj_send,
@@ -285,6 +285,15 @@
         for level in range(SUB):
             mem_lvl[sub * SUB + level, :, span] = mem_wide[sub, :, level, span]
 
+    eye = jnp.where(iota((DEPTH, DEPTH), 0) == iota((DEPTH, DEPTH), 1), 1.0, 0.0).astype(BF16)
+
+    def turn_blocks(group):
+        for level in range(0, levels, 2):
+            turned[group, level // 2] = lax.dot_general(
+                eye, blocks_of(group, level), (((1,), (1,)), ((), ())),
+                preferred_element_type=F32,
+            ).astype(BF16)
+
     finish(0)
     for sub in range(subs):
         for level in range(SUB):
@@ -294,6 +303,11 @@
     for c in range(1, len(chunks) - 1):
         finish(c)
         spread_members(c)
+        if c == 1:
+            loaded([late])
+        share = pl.cdiv(groups, len(chunks) - 2)
+        for group in range((c - 1) * share, min(c * share, groups)):
+            turn_blocks(group)
     per_lane = owners.shape[1] // blocks
     line = owners[pl.ds(lax.div(tile, per_lane), 1)]
     owner = line[:, :blocks]
@@ -310,26 +324,23 @@
     placing = jnp.where(iota((tiles * capacity, blocks), 0) == target, 1.0, 0.0)
     others = slice(0, tiles - 1)
 
-    def at_blocks(ref):
-        return lax.dot_general(
-            placing, ref[...].reshape(tiles * capacity, quarter), (((0,), (0,)), ((), ())),
-            precision=HIGHEST, preferred_element_type=F32,
-        )
-
-    loaded([late])
     finish(len(chunks) - 1)
+    spread_members(len(chunks) - 1)
     for sub in range(subs):
         for c in range(sub * SPANS, (sub + 1) * SPANS):
             if c == len(chunks) - 1:
-                spread_members(c)
                 loaded(range(late + 1, len(loads)))
                 await_bytes(innov.at[others], innov_recv)
                 await_bytes(obs.at[others], obs_recv)
-                innov_block = at_blocks(innov)
-                obs_block = at_blocks(obs)
+                at_blocks = lax.dot_general(
+                    placing, jnp.concatenate([
+                        ref[...].reshape(tiles * capacity, quarter) for ref in (innov, obs)
+                    ], axis=1), (((0,), (0,)), ((), ())),
+                    precision=HIGHEST, preferred_element_type=F32,
+                )
             gather(c)
         project(sub)
-    departure = obs_block * (innov_block - image[...])
+    departure = at_blocks[:, quarter:] * (at_blocks[:, :quarter] - image[...])
     image[...] = departure
 
     rounded = departure.astype(BF16)
@@ -340,10 +351,7 @@
             jnp.concatenate([own, blank], axis=1), jnp.concatenate([blank, own], axis=1)
         ], axis=0)
         for level in range(0, levels, 2):
-            value = lax.dot_general(
-                left, blocks_of(group, level), (((1,), (1,)), ((), ())),
-                preferred_element_type=F32,
-            )
+            value = jnp.dot(left, turned[group, level // 2], preferred_element_type=F32)
             for k in range(2):
                 upward[level + k : level + k + 1, group * DEPTH : (group + 1) * DEPTH] = jnp.sum(
                     jnp.where(diagonal, value[k * per_group : (k + 1) * per_group], 0.0),
@@ -424,9 +432,9 @@
         for t in range(1, tiles * CORES):
             value = value + terms[c * CORES + t // tiles, t % tiles]
         for k in range(2):
-            turned = value if k == 0 else pltpu.roll(value, LANES // 2, 1)
-            turned = jnp.where(lane < modes_chip, turned, 0.0)
-            whole[k] = whole[k] + (pltpu.roll(turned, c * modes_chip, 1) if c else turned)
+            moved = value if k == 0 else pltpu.roll(value, LANES // 2, 1)
+            moved = jnp.where(lane < modes_chip, moved, 0.0)
+            whole[k] = whole[k] + (pltpu.roll(moved, c * modes_chip, 1) if c else moved)
     whole = jnp.concatenate(whole, axis=0)
     grad_ref[...] = (
         control[pl.ds(pl.multiple_of(me * mem_dev, mem_dev), mem_dev)]
@@ -515,6 +523,7 @@
             pltpu.VMEM((total_members, LANES), F32),
             pltpu.VMEM((nband, mem_dev // 2, LANES), F32),
             pltpu.VMEM((nband, tiles, mem_dev // 2, LANES), F32),
+            pltpu.VMEM((blocks * patch // DEPTH, levels // 2, 2 * quarter, DEPTH), BF16),
             pltpu.SemaphoreType.REGULAR((rounds,)),
             dma(8), dma(subs), dma(subs), dma(subs * SPANS), dma(subs * SPANS), dma(SPANS),
             *[dma() for _ in range(13)],

time: 34.7 us -> 34 us (0.980)
  Pallas kernels: 33.9 us -> 33.2 us
    pallas_call x1, Pallas kernels: 33.2 us -> 32.5 us  [per_device(): pl.pallas_call(functools.partial(whole_kernel, nband, tiles, scale), out_...]
where the time goes in v5:
time: 34 us; the launch traced here: 33.9 us
  Pallas kernels  33.2 us (98%)
  between operations  0.64 us (2%)
    pallas_call x1, Pallas kernels, per_device(): pl.pallas_call(functools.partial(whole_kernel, nband, tiles, scale), out_...  32.5 us

profile of v5, /device:TPU:0, one launch (start us, length us, event | category | flops | bytes accessed | tf_op | source)
XLA Modules:
  0.0 33.9 jit_solution(11628423016675939316)
XLA Ops:
  0.6 32.5 %shard_map.95 = (f32[16,112]{1,0:T(8,128)S(1)}, f32[1,256,128]{2,1,0:T(8,128)S(1)}) custom-call(bf16[16,16,1024]{2,1,0:T(8,128)(2,1)} %mem_hbm.1, bf16[28,16,1024]{2,1,0:T(8,128)(2,1)} %eig_hbm.1, f32[64,112]{1,0:T(8,128)} %bitcast.4, s32[16,64]{1,0:T(8,128)} %bitcast.5, bf16[64,256,512]{2,1,0:T(8,128)(2,1)} %interp_hbm.1, s32[4,128]{1,0:T(4,128)} %bitcast.6, ...), custom_call_target="tpu_custom_call" | custom-call | tf_op jit(solution)/shard_map/pallas_call | solution.py:492
  33.2 0.7 %shard_map.96 = (f32[16,112]{1,0:T(8,128)}, f32[1,256,128]{2,1,0:T(8,128)}) custom-call(f32[16,112]{1,0:T(8,128)S(1)} %get-tuple-element.6.grad_ref, f32[1,256,128]{2,1,0:T(8,128)S(1)} %get-tuple-element.7.dep_ref), custom_call_target="tpu_custom_call" | custom-call | tf_op jit(solution)/shard_map/pallas_call | solution.py:536

commit v6 on v5

--- a/solution.py
+++ b/solution.py
@@ -410,9 +410,9 @@
     local[:, :modes_chip] = total
     rows = mem_dev // 2
     for b in range(nband):
-        packed[b] = local[b * mem_dev : b * mem_dev + rows] + pltpu.roll(
+        packed[b] = (local[b * mem_dev : b * mem_dev + rows] + pltpu.roll(
             local[b * mem_dev + rows : (b + 1) * mem_dev], LANES // 2, 1
-        )
+        )).astype(BF16)
     for far in range(tiles - 1, -1, -1):
         for step in range(nband - 1, -1, -1):
             if far or step:
@@ -428,9 +428,9 @@
     whole = [jnp.zeros((rows, LANES), F32)] * 2
     lane = iota((rows, LANES), 1)
     for c in range(chips):
-        value = terms[c * CORES, 0]
+        value = terms[c * CORES, 0].astype(F32)
         for t in range(1, tiles * CORES):
-            value = value + terms[c * CORES + t // tiles, t % tiles]
+            value = value + terms[c * CORES + t // tiles, t % tiles].astype(F32)
         for k in range(2):
             moved = value if k == 0 else pltpu.roll(value, LANES // 2, 1)
             moved = jnp.where(lane < modes_chip, moved, 0.0)
@@ -521,8 +521,8 @@
             pltpu.VMEM((CORES, levels, half), F32),
             pltpu.VMEM((nband - 1, levels, half), F32),
             pltpu.VMEM((total_members, LANES), F32),
-            pltpu.VMEM((nband, mem_dev // 2, LANES), F32),
-            pltpu.VMEM((nband, tiles, mem_dev // 2, LANES), F32),
+            pltpu.VMEM((nband, mem_dev // 2, LANES), BF16),
+            pltpu.VMEM((nband, tiles, mem_dev // 2, LANES), BF16),
             pltpu.VMEM((blocks * patch // DEPTH, levels // 2, 2 * quarter, DEPTH), BF16),
             pltpu.SemaphoreType.REGULAR((rounds,)),
             dma(8), dma(subs), dma(subs), dma(subs * SPANS), dma(subs * SPANS), dma(SPANS),

time: 34 us -> 33.2 us (0.976)
  Pallas kernels: 33.2 us -> 32.4 us
    pallas_call x1, Pallas kernels: 32.5 us -> 31.8 us  [per_device(): pl.pallas_call(functools.partial(whole_kernel, nband, tiles, scale), out_...]
where the time goes in v6:
time: 33.2 us; the launch traced here: 33.1 us
  Pallas kernels  32.4 us (98%)
  between operations  0.64 us (2%)
    pallas_call x1, Pallas kernels, per_device(): pl.pallas_call(functools.partial(whole_kernel, nband, tiles, scale), out_...  31.8 us
    pallas_call x1, Pallas kernels, per_device(): pl.pallas_call(write_out, out_shape=tuple((jax.ShapeDtypeStruct(x.shape,...  0.68 us

profile of v6, /device:TPU:0, one launch (start us, length us, event | category | flops | bytes accessed | tf_op | source)
XLA Modules:
  0.0 33.1 jit_solution(18034919212006968487)
XLA Ops:
  0.6 31.8 %shard_map.95 = (f32[16,112]{1,0:T(8,128)S(1)}, f32[1,256,128]{2,1,0:T(8,128)S(1)}) custom-call(bf16[16,16,1024]{2,1,0:T(8,128)(2,1)} %mem_hbm.1, bf16[28,16,1024]{2,1,0:T(8,128)(2,1)} %eig_hbm.1, f32[64,112]{1,0:T(8,128)} %bitcast.4, s32[16,64]{1,0:T(8,128)} %bitcast.5, bf16[64,256,512]{2,1,0:T(8,128)(2,1)} %interp_hbm.1, s32[4,128]{1,0:T(4,128)} %bitcast.6, ...), custom_call_target="tpu_custom_call" | custom-call | tf_op jit(solution)/shard_map/pallas_call | solution.py:492
  32.4 0.7 %shard_map.96 = (f32[16,112]{1,0:T(8,128)}, f32[1,256,128]{2,1,0:T(8,128)}) custom-call(f32[16,112]{1,0:T(8,128)S(1)} %get-tuple-element.6.grad_ref, f32[1,256,128]{2,1,0:T(8,128)S(1)} %get-tuple-element.7.dep_ref), custom_call_target="tpu_custom_call" | custom-call | tf_op jit(solution)/shard_map/pallas_call | solution.py:536
